TPU v7x, 128 devices: a whole 4x4x4 slice. The times are simulated.
128 devices in a mesh: gx: 4 (over z), gz: 16 (over x, y), gy: 2 (over core).
Axes of the slice: x: 4, y: 4, z: 4, core: 2. Of those that a mesh axis runs over, the one named last changes fastest.
Arguments:
- velocity: float32 [3, 128, 192, 2048], P(None, ('gx', 'gy'), None, 'gz'), may hold values from -6 to 6
- metric_x: float32 [128], P(('gx', 'gy')), may hold values from 0.5 to 2
- metric_y: float32 [192], replicated, may hold values from 0.5 to 2
- metric_z: float32 [2048], P('gz'), may hold values from 0.5 to 2
- x_inverse: float32 [128, 16], P(('gx', 'gy')), may hold values from -5 to 5, as said below
- y_inverse: float32 [192, 192], replicated, may hold values from -5 to 5, as said below
- z_inverse: float32 [2048, 128], P('gz'), may hold values from -5 to 5, as said below
Outputs:
- gradient: float32 [3, 3, 128, 192, 2048], P(None, None, ('gx', 'gy'), None, 'gz')
- convection: float32 [3, 128, 192, 2048], P(None, ('gx', 'gy'), None, 'gz')
Inputs may be any that keep to these rules, and one draw needn't show every extreme that they name: Rows b * 16 to b * 16 + 15 of x_inverse hold the inverse of a 16 x 16 tridiagonal matrix with unit diagonal whose row r has one value between 0.2 and 0.4 on both sides of the diagonal (where they exist), drawn afresh for each row and block. y_inverse holds the inverse of such a 192 x 192 matrix. Likewise for z_inverse with blocks of 128 rows.
All inputs are finite; a program needn't handle non-finite values.
Results may differ from a plain program's by a relative error of at most 0.0003.
Values sent between devices are 32-bit elements; how exact they have to be, the bound alone decides.
A program may use at most 192 MiB of HBM per device.

v0:
```python
import jax
import jax.numpy as jnp
from jax import lax
from jax.sharding import PartitionSpec as P

COUPLING = 1.0 / 3.0
NEAR_WEIGHT = 7.0 / 9.0
FAR_WEIGHT = 1.0 / 36.0


def with_halo(shard, sides, width):
    edges = {}
    for axis, dim in sides:
        devices, length = (lax.axis_size(axis), shard.shape[dim])
        up = [(i, (i + 1) % devices) for i in range(devices)]
        last = lax.slice_in_dim(shard, length - width, length, axis=dim)
        first = lax.slice_in_dim(shard, 0, width, axis=dim)
        edges[dim] = (
            lax.ppermute(last, axis, up),
            lax.ppermute(first, axis, [(b, a) for a, b in up]),
        )
    done = []
    for _, dim in sides:
        low, high = edges[dim]
        around = [(width, width) if d in done else (0, 0) for d in range(shard.ndim)]
        shard = jnp.concatenate([jnp.pad(low, around), shard, jnp.pad(high, around)], axis=dim)
        done.append(dim)
    return shard


def padded_2(cells, sides, width):
    for axis, dim in sides:
        count = lax.axis_size(axis)
        head = lax.slice_in_dim(cells, 0, width, axis=dim)
        tail = lax.slice_in_dim(cells, cells.shape[dim] - width, cells.shape[dim], axis=dim)
        cells = jnp.concatenate(
            [
                lax.ppermute(tail, axis, [(i, (i + 1) % count) for i in range(count)]),
                cells,
                lax.ppermute(head, axis, [((i + 1) % count, i) for i in range(count)]),
            ],
            axis=dim,
        )
    return cells


def direction_fields(velocity, direction):
    return jnp.concatenate([velocity, velocity * velocity[direction : direction + 1]], axis=0)


def stencil(padded, axis_of, length):

    def shifted(offset):
        return lax.slice_in_dim(padded, 2 + offset, 2 + offset + length, axis=axis_of)

    return NEAR_WEIGHT * (shifted(1) - shifted(-1)) + FAR_WEIGHT * (shifted(2) - shifted(-2))


def block_solve(source, inverse, axis_of):
    if axis_of == 1:
        form = "ij,fjyz->fiyz"
    elif axis_of == 2:
        form = "ij,fxjz->fxiz"
    else:
        form = "ij,fxyj->fxyi"
    return jnp.einsum(form, inverse, source, precision=lax.Precision.HIGHEST)


def pick(values, position, axis_of):
    return lax.slice_in_dim(values, position, position + 1, axis=axis_of)


def end_rows(inside, inverse, axis_of):
    length = inside.shape[axis_of]
    edges = jnp.concatenate(
        [pick(inside, 0, axis_of), pick(inside, length - 1, axis_of)], axis=axis_of
    )
    layout = [1, 1, 1, 1]
    layout[axis_of] = 2
    corner = jnp.stack([inverse[0, 0], inverse[length - 1, length - 1]]).reshape(layout)
    corner = jnp.broadcast_to(corner, (1,) + edges.shape[1:])
    return jnp.concatenate([edges, corner], axis=0)


def combine_ends(inside, nearby, inverse, axis_of):
    fields = inside.shape[0]
    values = nearby[:fields]
    corners = nearby[fields:]
    left_value = pick(values, 0, axis_of)
    left_tail = pick(corners, 0, axis_of)
    own_head = pick(values, 1, axis_of)
    own_first = pick(corners, 1, axis_of)
    own_tail = pick(values, 2, axis_of)
    own_last = pick(corners, 2, axis_of)
    right_value = pick(values, 3, axis_of)
    right_first = pick(corners, 3, axis_of)
    left_final = (left_value - COUPLING * left_tail * own_head) / (
        1.0 - COUPLING * COUPLING * left_tail * own_first
    )
    right_start = (right_value - COUPLING * right_first * own_tail) / (
        1.0 - COUPLING * COUPLING * own_last * right_first
    )
    length = inverse.shape[0]
    layout = [1, 1, 1, 1]
    layout[axis_of] = length
    column_first = inverse[:, 0].reshape(layout)
    column_last = inverse[:, length - 1].reshape(layout)
    return inside - COUPLING * column_first * left_final - COUPLING * column_last * right_start


def on_device(velocity, metric_x, metric_y, metric_z, x_inverse, y_inverse, z_inverse):
    count_x = velocity.shape[1]
    count_y = velocity.shape[2]
    count_z = velocity.shape[3]
    plane_rim = with_halo(velocity, ((("gx", "gy"), 1), ("gz", 3)), 2)
    wide_x = direction_fields(plane_rim[:, :, :, 2 : 2 + count_z], 0)
    wide_z = direction_fields(plane_rim[:, 2 : 2 + count_x], 2)
    wide_y = jnp.pad(direction_fields(velocity, 1), ((0, 0), (0, 0), (2, 2), (0, 0)))
    inside_x = block_solve(stencil(wide_x, 1, count_x), x_inverse, 1)
    nearby_x = with_halo(end_rows(inside_x, x_inverse, 1), ((("gx", "gy"), 1),), 1)
    result_x = combine_ends(inside_x, nearby_x, x_inverse, 1) * metric_x.reshape(1, count_x, 1, 1)
    result_y = block_solve(stencil(wide_y, 2, count_y), y_inverse, 2) * metric_y.reshape(
        1, 1, count_y, 1
    )
    inside_z = block_solve(stencil(wide_z, 3, count_z), z_inverse, 3)
    nearby_z = padded_2(end_rows(inside_z, z_inverse, 3), (("gz", 3),), 1)
    result_z = combine_ends(inside_z, nearby_z, z_inverse, 3) * metric_z.reshape(1, 1, 1, count_z)
    gradient = jnp.stack([result_x[:3], result_y[:3], result_z[:3]], axis=1)
    convection = result_x[3:] + result_y[3:] + result_z[3:]
    return (gradient, convection)


def solution(mesh):
    return jax.shard_map(
        on_device,
        mesh=mesh,
        in_specs=(
            P(None, ("gx", "gy"), None, "gz"),
            P(("gx", "gy")),
            P(),
            P("gz"),
            P(("gx", "gy"), None),
            P(),
            P("gz", None),
        ),
        out_specs=(P(None, None, ("gx", "gy"), None, "gz"), P(None, ("gx", "gy"), None, "gz")),
        check_vma=False,
    )
```

profile of v0, /device:TPU:0, one launch (start us, length us, event | category | flops | bytes accessed | tf_op | source)
XLA Modules:
  0.0 352.8 jit_solution(16002979591250252444)
XLA Ops:
  0.6 8.9 %fusion.55 = (f32[3,16,192,2]{3,2,1,0:T(8,128)}, f32[3,16,192,2]{3,2,1,0:T(8,128)}) fusion(f32[3,16,192,128]{3,2,1,0:T(8,128)} %param.7), kind=kLoop, calls=%fused_computation.111 | loop fusion | bytes 294912 | tf_op jit(solution)/shard_map/slice | solution.py:16
  9.6 3.5 copy.48
  13.1 5.4 %collective-permute-start.5 = (f32[3,16,192,2]{2,1,3,0:T(8,128)S(1)}, f32[3,16,192,2]{2,1,3,0:T(8,128)S(1)}, u32[]{:S(2)}, u32[]{:S(2)}) collective-permute-start(f32[3,16,192,2]{2,1,3,0:T(8,128)S(1)} %copy.48), channel_id=1, source_target_pairs={{2,0},{4,2},{6,4},{8,6},{10,8},{12,10},{14,12},{16,14},{18,16},{20... | collective-permute-start | bytes 221192 | tf_op jit(solution)/shard_map/ppermute | solution.py:20
  18.5 3.5 copy.47
  22.2 2.1 fusion.54
  24.4 3.2 collective-permute-start.1
  32.1 1.9 pad_maximum_fusion.7
  34.7 1.5 slice_bitcast_fusion.5
  36.3 1.8 pad_maximum_fusion.6
  38.1 3.0 copy.52
  41.1 3.0 copy.51
  44.0 1.3 constant_dynamic-update-slice_fusion.2
  45.3 5.7 %broadcast_multiply_fusion.2 = (f32[3,16,192,128]{3,2,1,0:T(8,128)}, f32[3,20,192,128]{3,2,1,0:T(8,128)S(1)}) fusion(f32[3,16,192,128]{3,2,1,0:T(8,128)} %param.7, f32[16,192,128]{2,1,0:T(8,128)S(1)} %slice_bitcast_fusion.5, f32[3,20,192,128]{3,2,1,0:T(8,128)S(1)} %constant_dynamic-update-slice_fusion.2), kind=kLoop, calls=%fused_computation.72 | loop fusion | flops 1179648 | bytes 15728640 | tf_op jit(solution)/shard_map/mul | solution.py:48
  51.0 1.1 constant_dynamic-update-slice_fusion
  52.1 1.6 slice_bitcast_fusion.4
  53.7 7.0 %select_maximum_fusion = f32[3,20,192,132]{3,2,1,0:T(8,128)S(1)} fusion(f32[3,16,192,2]{3,2,1,0:T(8,128)S(1)} %bitcast.58, f32[3,16,192,2]{3,2,1,0:T(8,128)} %copy.51, f32[3,20,192,128]{3,2,1,0:T(8,128)S(1)} %constant_dynamic-update-slice_fusion), kind=kLoop, calls=%fused_computation.15 | loop fusion | flops 9123840 | bytes 12128256 | tf_op jit(solution)/shard_map/concatenate | solution.py:26
  61.0 7.7 %broadcast_multiply_fusion = (f32[3,16,192,132]{3,2,1,0:T(8,128)}, f32[3,16,192,132]{3,2,1,0:T(8,128)}) fusion(f32[16,192,132]{2,1,0:T(8,128)S(1)} %slice_bitcast_fusion.3, f32[3,20,192,132]{3,2,1,0:T(8,128)S(1)} %select_maximum_fusion), kind=kLoop, calls=%fused_computation.64 | loop fusion | flops 1216512 | bytes 16220160 | tf_op jit(solution)/shard_map/mul | solution.py:48
  68.8 27.7 %fusion.13 = f32[6,16,192,128]{3,2,1,0:T(8,128)} fusion(f32[3,16,192,132]{3,2,1,0:T(8,128)} %get-tuple-element.13, f32[3,16,192,132]{3,2,1,0:T(8,128)} %get-tuple-element.12, f32[128,128]{1,0:T(8,128)S(1)} %copy-done.5), kind=kOutput, calls=%fused_computation.33 | convolution fusion | flops 3645112320 | bytes 19234816 | tf_op jit(solution)/shard_map/ij,fxyj->fxyi/dot_general | solution.py:66
  96.4 14.8 %fusion.53 = (f32[6,16,192,1]{3,2,1,0:T(8,128)}, f32[6,16,192,1]{3,2,1,0:T(8,128)}) fusion(f32[6,16,192,128]{3,2,1,0:T(8,128)} %fusion.13), kind=kLoop, calls=%fused_computation.109 | loop fusion | bytes 294912 | tf_op jit(solution)/shard_map/slice | solution.py:70
  111.2 6.3 %copy.30 = f32[6,16,192,1]{2,1,3,0:T(8,128)S(1)} copy(f32[6,16,192,1]{3,2,1,0:T(8,128)} %get-tuple-element.23) | data formatting | bytes 147456 | tf_op jit(solution)/shard_map/slice | solution.py:70
  117.4 6.4 %copy.29 = f32[6,16,192,1]{2,1,3,0:T(8,128)S(1)} copy(f32[6,16,192,1]{3,2,1,0:T(8,128)} %get-tuple-element.22) | data formatting | bytes 147456 | tf_op jit(solution)/shard_map/slice | solution.py:70
  124.7 5.1 %collective-permute-start.7 = (f32[7,16,192,1]{2,1,3,0:T(8,128)}, f32[7,16,192,1]{2,1,3,0:T(8,128)}, u32[]{:S(2)}, u32[]{:S(2)}) collective-permute-start(f32[7,16,192,1]{2,1,3,0:T(8,128)} %get-tuple-element.37), channel_id=1, source_target_pairs={{2,0},{4,2},{6,4},{8,6},{10,8},{12,10},{14,12},{16,14},{18,16},{20... | collective-permute-start | bytes 258056 | tf_op jit(solution)/shard_map/ppermute | solution.py:40
  130.0 8.9 %select_maximum_fusion.2 = f32[6,16,196,128]{3,2,1,0:T(8,128)} fusion(f32[3,16,192,128]{3,2,1,0:T(8,128)} %get-tuple-element.24, f32[3,16,192,128]{3,2,1,0:T(8,128)} %param.7), kind=kLoop, calls=%fused_computation.19 | loop fusion | flops 14450688 | bytes 19070976 | tf_op jit(solution)/shard_map/concatenate | solution.py:48
  138.8 4.6 %broadcast_multiply_fusion.1 = f32[3,20,192,128]{3,2,1,0:T(8,128)} fusion(f32[3,20,192,128]{3,2,1,0:T(8,128)S(1)} %bitcast.56, f32[20,192,128]{2,1,0:T(8,128)} %slice_bitcast_fusion.4), kind=kLoop, calls=%fused_computation.71 | loop fusion | flops 1474560 | bytes 13762560 | tf_op jit(solution)/shard_map/mul | solution.py:48
  143.5 13.5 %fusion.4 = f32[6,16,192,128]{3,2,1,0:T(8,128)} fusion(f32[3,20,192,128]{3,2,1,0:T(8,128)S(1)} %bitcast.56, f32[3,20,192,128]{3,2,1,0:T(8,128)} %broadcast_multiply_fusion.1), kind=kLoop, calls=%fused_computation.24 | loop fusion | flops 21233664 | bytes 21233664 | tf_op jit(solution)/shard_map/add | solution.py:56
  157.0 17.6 %fusion.39 = f32[6,16,192,128]{3,1,2,0:T(8,128)S(1)} fusion(f32[6,16,192,128]{3,2,1,0:T(8,128)} %fusion.4, f32[16,16]{1,0:T(8,128)S(1)} %copy-done.7), kind=kOutput, calls=%fused_computation.69 | convolution fusion | flops 452984832 | bytes 18875392 | tf_op jit(solution)/shard_map/ij,fjyz->fiyz/dot_general | solution.py:66
  174.6 3.6 %copy-done.2 = f32[6,16,192,128]{3,1,2,0:T(8,128)} copy-done((f32[6,16,192,128]{3,1,2,0:T(8,128)}, f32[6,16,192,128]{3,1,2,0:T(8,128)S(1)}, u32[]{:S(2)}) %copy-start.2) | copy-done | bytes 9437208
  179.2 1.1 pad_maximum_fusion.4
  180.4 1.3 fusion.56
  181.7 2.9 collective-permute-start.3
  184.6 23.8 %fusion.24 = f32[6,16,128,192]{2,3,1,0:T(8,128)} fusion(f32[6,16,196,128]{3,2,1,0:T(8,128)} %select_maximum_fusion.2, f32[192,192]{1,0:T(8,128)S(1)} %copy-done), kind=kOutput, calls=%fused_computation.43 | convolution fusion | flops 5447614464 | bytes 47333376 | tf_op jit(solution)/shard_map/ij,fxjz->fxiz/dot_general | solution.py:66
  208.4 14.5 %fusion.32 = f32[6,16,192,128]{3,1,2,0:T(8,128)} fusion(f32[6,16,128,192]{2,3,1,0:T(8,128)} %fusion.24, f32[192]{0:T(256)S(1)} %copy-done.11), kind=kLoop, calls=%fused_computation.53 | loop fusion | flops 2359296 | bytes 18875136 | tf_op jit(solution)/shard_map/mul | solution.py:122
  224.5 5.1 %copy.38 = f32[6,16,192,1]{3,2,1,0:T(8,128)} copy(f32[6,16,192,1]{2,1,3,0:T(8,128)S(1)} %slice_subtract_fusion.4) | data formatting | bytes 147456 | tf_op jit(solution)/shard_map/sub | solution.py:100
  229.7 9.4 %broadcast_divide_fusion = f32[6,16,192,1]{3,2,1,0:T(8,128)} fusion(f32[6,16,192,1]{3,2,1,0:T(8,128)} %copy.38, f32[16,192]{1,0:T(8,128)S(1)} %get-tuple-element.40), kind=kLoop, calls=%fused_computation.62 | loop fusion | flops 18432 | bytes 159744 | tf_op jit(solution)/shard_map/div | solution.py:100
  239.1 8.7 %copy.46 = f32[6,16,192,1]{1,2,0,3:T(8,128)S(1)} copy(f32[6,16,192,1]{3,2,1,0:T(8,128)} %broadcast_divide_fusion) | data formatting | bytes 147456 | tf_op jit(solution)/shard_map/mul | solution.py:108
  248.6 0.9 slice_subtract_fusion.5
  249.5 5.1 %copy.33 = f32[6,16,192,1]{3,2,1,0:T(8,128)} copy(f32[6,16,192,1]{2,1,3,0:T(8,128)S(1)} %slice_subtract_fusion.5) | data formatting | bytes 147456 | tf_op jit(solution)/shard_map/sub | solution.py:97
  254.6 9.4 %broadcast_divide_fusion.1 = f32[6,16,192,1]{3,2,1,0:T(8,128)} fusion(f32[6,16,192,1]{3,2,1,0:T(8,128)} %copy.33, f32[16,192]{1,0:T(8,128)S(1)} %get-tuple-element.38), kind=kLoop, calls=%fused_computation.63 | loop fusion | flops 18432 | bytes 159744 | tf_op jit(solution)/shard_map/div | solution.py:97
  264.1 8.9 %copy.45 = f32[6,16,192,1]{1,2,0,3:T(8,128)S(1)} copy(f32[6,16,192,1]{3,2,1,0:T(8,128)} %broadcast_divide_fusion.1) | data formatting | bytes 147456 | tf_op jit(solution)/shard_map/mul | solution.py:108
  273.0 14.0 %fusion.31 = f32[6,16,192,128]{3,1,2,0:T(8,128)} fusion(f32[6,16,192,128]{3,2,1,0:T(8,128)} %fusion.13, f32[128]{0:T(128)S(1)} %copy-done.12, f32[6,16,192]{1,2,0:T(8,128)S(1)} %bitcast.59, f32[128]{0:T(128)S(1)} %copy-done.8, f32[6,16,192]{1,2,0:T(8,128)S(1)} %bitcast.60, f32[128]{0:T(128)S(1)} %get-tuple-element.8), kind=kLoop, calls=%fused_computation.51 | loop fusion | flops 11796480 | bytes 19023360 | tf_op jit(solution)/shard_map/mul | solution.py:127
  287.1 1.1 slice_multiply_fusion.1
  288.2 1.1 slice_multiply_fusion
  289.2 5.0 %fusion.43 = (f32[6,1,192,128]{3,1,2,0:T(1,128)S(1)}, f32[6,1,192,128]{3,1,2,0:T(1,128)S(1)}) fusion(f32[7,1,192,128]{3,1,2,0:T(1,128)} %collective-permute-done.2, f32[192,128]{1,0:T(8,128)S(1)} %bitcast.64, f32[192,128]{1,0:T(8,128)S(1)} %bitcast.63, f32[6,16,192,128]{3,1,2,0:T(8,128)} %copy-done.2, f32[192,128]{1,0:T(8,128)S(1)} %bitcast.66, ...), kind=kLoop, calls=%fused_computation.79 | loop fusion | flops 884736 | bytes 3932160 | tf_op jit(solution)/shard_map/div | solution.py:97
  294.3 9.2 %subtract_multiply_fusion = f32[6,16,192,128]{3,1,2,0:T(8,128)} fusion(f32[6,16,192,128]{3,1,2,0:T(8,128)} %copy-done.2, f32[16]{0:T(128)S(1)} %copy-done.13, f32[6,192,128]{2,1,0:T(8,128)S(1)} %bitcast.62, f32[16]{0:T(128)S(1)} %copy-done.10, f32[6,192,128]{2,1,0:T(8,128)S(1)} %bitcast.61, f32[16]{0:T(128)S(1)} %copy-done.9), kind=kLoop, calls=%fused_computation.56 | loop fusion | flops 11796480 | bytes 20054208 | tf_op jit(solution)/shard_map/mul | solution.py:121
  303.4 17.4 %slice_add_fusion = (f32[3,16,192,128]{3,1,2,0:T(8,128)}, f32[3,1,16,192,128]{4,2,3,0,1:T(8,128)}, f32[3,1,16,192,128]{4,2,3,0,1:T(8,128)}, f32[3,1,16,192,128]{4,2,3,0,1:T(8,128)}) fusion(f32[6,16,192,128]{3,1,2,0:T(8,128)} %fusion.31, f32[6,16,192,128]{3,1,2,0:T(8,128)} %fusion.32, f32[6,16,192,128]{3,1,2,0:T(8,128)} %subtract_multiply_fusion), kind=kLoop, calls=%fused_computation.57 | loop fusion | flops 2359296 | bytes 47185920 | tf_op jit(solution)/shard_map/add | solution.py:129
  320.9 11.1 %pad_maximum_fusion = f32[3,3,16,192,128]{4,2,3,0,1:T(8,128)} fusion(f32[3,1,16,192,128]{4,2,3,0,1:T(8,128)} %get-tuple-element.17, f32[3,1,16,192,128]{4,2,3,0,1:T(8,128)} %get-tuple-element.16, f32[3,1,16,192,128]{4,2,3,0,1:T(8,128)} %get-tuple-element.15), kind=kLoop, calls=%fused_computation.14 | loop fusion | flops 7077888 | bytes 28311552 | tf_op jit(solution)/shard_map/stack | solution.py:128
  332.0 14.6 %copy.40 = f32[3,3,16,192,128]{4,3,2,1,0:T(8,128)} copy(f32[3,3,16,192,128]{4,2,3,0,1:T(8,128)} %pad_maximum_fusion) | data formatting | bytes 28311552
  346.6 5.9 %copy.41 = f32[3,16,192,128]{3,2,1,0:T(8,128)} copy(f32[3,16,192,128]{3,1,2,0:T(8,128)} %get-tuple-element.14) | data formatting | bytes 9437184
  (66 shorter events, 7.8 us)
Async XLA Ops:
  0.6 184.0 %copy-start = (f32[192,192]{1,0:T(8,128)S(1)}, f32[192,192]{1,0:T(8,128)}, u32[]{:S(2)}) copy-start(f32[192,192]{1,0:T(8,128)} %param.12) | copy-start | bytes 442372
  9.6 18.0 %copy-start.6 = (f32[16,16]{1,0:T(8,128)S(1)}, f32[16,16]{1,0:T(8,128)}, u32[]{:S(2)}) copy-start(f32[16,16]{1,0:T(8,128)} %param.11) | copy-start | bytes 3076
  9.6 19.4 %copy-start.4 = (f32[128,128]{1,0:T(8,128)S(1)}, f32[128,128]{1,0:T(8,128)}, u32[]{:S(2)}) copy-start(f32[128,128]{1,0:T(8,128)} %param.13) | copy-start | bytes 196612
  13.1 25.0 %collective-permute-start.5 = (f32[3,16,192,2]{2,1,3,0:T(8,128)S(1)}, f32[3,16,192,2]{2,1,3,0:T(8,128)S(1)}, u32[]{:S(2)}, u32[]{:S(2)}) collective-permute-start(f32[3,16,192,2]{2,1,3,0:T(8,128)S(1)} %copy.48), channel_id=1, source_target_pairs={{2,0},{4,2},{6,4},{8,6},{10,8},{12,10},{14,12},{16,14},{18,16},{20... | collective-permute-start | bytes 221192 | tf_op jit(solution)/shard_map/ppermute | solution.py:20
  22.0 19.1 %collective-permute-start.4 = (f32[3,16,192,2]{2,1,3,0:T(8,128)S(1)}, f32[3,16,192,2]{2,1,3,0:T(8,128)S(1)}, u32[]{:S(2)}, u32[]{:S(2)}) collective-permute-start(f32[3,16,192,2]{2,1,3,0:T(8,128)S(1)} %copy.47), channel_id=1, source_target_pairs={{0,2},{2,4},{4,6},{6,8},{8,10},{10,12},{12,14},{14,16},{16,18},{18... | collective-permute-start | bytes 221192 | tf_op jit(solution)/shard_map/ppermute | solution.py:19
  24.4 19.7 %collective-permute-start = (f32[3,2,192,128]{3,2,1,0:T(8,128)S(1)}, f32[3,2,192,128]{3,2,1,0:T(8,128)}, u32[]{:S(2)}, u32[]{:S(2)}) collective-permute-start(f32[3,2,192,128]{3,2,1,0:T(8,128)S(1)} %get-tuple-element.27), channel_id=1, source_target_pairs={{0,1},{1,32},{32,33},{33,64},{64,65},{65,96},{96,97},{97,0},{2,3},... | collective-permute-start | bytes 1769480 | tf_op jit(solution)/shard_map/ppermute | solution.py:19
  24.4 26.6 %collective-permute-start.1 = (f32[3,2,192,128]{3,2,1,0:T(8,128)}, f32[3,2,192,128]{3,2,1,0:T(8,128)}, u32[]{:S(2)}, u32[]{:S(2)}) collective-permute-start(f32[3,2,192,128]{3,2,1,0:T(8,128)} %get-tuple-element.26), channel_id=1, source_target_pairs={{1,0},{32,1},{33,32},{64,33},{65,64},{96,65},{97,96},{0,97},{3,2},... | collective-permute-start | bytes 1769480 | tf_op jit(solution)/shard_map/ppermute | solution.py:20
  44.0 9.7 %slice-start.2 = ((s8[4718592]{0:T(1024)(128)(4,1)}), s8[4194304]{0:T(1024)(128)(4,1)S(1)}, s32[]{:S(2)}) async-start(s8[4718592]{0:T(1024)(128)(4,1)} %bitcast.57), calls=%async_computation.2 | async-start | bytes 8388608
  45.3 8.4 %slice-start.3 = ((s8[4718592]{0:T(1024)(128)(4,1)}), s8[524288]{0:T(1024)(128)(4,1)S(1)}, s32[]{:S(2)}) async-start(s8[4718592]{0:T(1024)(128)(4,1)} %bitcast.57), calls=%async_computation.3 | async-start | bytes 1048576
  52.1 8.6 %copy-start.3 = (f32[3,20,192,128]{3,2,1,0:T(8,128)}, f32[3,20,192,128]{3,2,1,0:T(8,128)S(1)}, u32[]{:S(2)}) copy-start(f32[3,20,192,128]{3,2,1,0:T(8,128)S(1)} %constant_dynamic-update-slice_fusion) | copy-start | bytes 17694724
  61.0 7.7 %copy-start.5 = (f32[128,128]{1,0:T(8,128)S(1)}, f32[128,128]{1,0:T(8,128)}, u32[]{:S(2)}) copy-start(f32[128,128]{1,0:T(8,128)} %param.13) | copy-start | bytes 196612
  111.2 12.7 %copy-start.15 = (f32[2]{0:T(128)S(1)}, f32[2]{0:T(128)}, u32[]{:S(2)}) copy-start(f32[2]{0:T(128)} %pad_maximum_fusion.7) | copy-start | bytes 28
  117.4 21.4 %slice-start = ((s8[5898240]{0:T(1024)(128)(4,1)}), s8[1703936]{0:T(1024)(128)(4,1)S(1)}, s32[]{:S(2)}) async-start(s8[5898240]{0:T(1024)(128)(4,1)} %bitcast.55), calls=%async_computation | async-start | bytes 3407872
  124.7 98.3 %collective-permute-start.7 = (f32[7,16,192,1]{2,1,3,0:T(8,128)}, f32[7,16,192,1]{2,1,3,0:T(8,128)}, u32[]{:S(2)}, u32[]{:S(2)}) collective-permute-start(f32[7,16,192,1]{2,1,3,0:T(8,128)} %get-tuple-element.37), channel_id=1, source_target_pairs={{2,0},{4,2},{6,4},{8,6},{10,8},{12,10},{14,12},{16,14},{18,16},{20... | collective-permute-start | bytes 258056 | tf_op jit(solution)/shard_map/ppermute | solution.py:40
  129.7 118.1 %collective-permute-start.6 = (f32[7,16,192,1]{2,1,3,0:T(8,128)}, f32[7,16,192,1]{2,1,3,0:T(8,128)}, u32[]{:S(2)}, u32[]{:S(2)}) collective-permute-start(f32[7,16,192,1]{2,1,3,0:T(8,128)} %get-tuple-element.36), channel_id=1, source_target_pairs={{0,2},{2,4},{4,6},{6,8},{8,10},{10,12},{12,14},{14,16},{16,18},{18... | collective-permute-start | bytes 258056 | tf_op jit(solution)/shard_map/ppermute | solution.py:38
  130.0 8.9 %slice-start.1 = ((s8[5898240]{0:T(1024)(128)(4,1)}), s8[4194304]{0:T(1024)(128)(4,1)S(1)}, s32[]{:S(2)}) async-start(s8[5898240]{0:T(1024)(128)(4,1)} %bitcast.55), calls=%async_computation.1 | async-start | bytes 8388608
  143.5 13.5 %copy-start.7 = (f32[16,16]{1,0:T(8,128)S(1)}, f32[16,16]{1,0:T(8,128)}, u32[]{:S(2)}) copy-start(f32[16,16]{1,0:T(8,128)} %param.11) | copy-start | bytes 3076
  157.0 22.1 %copy-start.14 = (f32[2]{0:T(128)S(1)}, f32[2]{0:T(128)}, u32[]{:S(2)}) copy-start(f32[2]{0:T(128)} %pad_maximum_fusion.6) | copy-start | bytes 28
  174.6 3.6 %copy-start.2 = (f32[6,16,192,128]{3,1,2,0:T(8,128)}, f32[6,16,192,128]{3,1,2,0:T(8,128)S(1)}, u32[]{:S(2)}) copy-start(f32[6,16,192,128]{3,1,2,0:T(8,128)S(1)} %fusion.39) | copy-start | bytes 28311556
  181.7 105.4 %collective-permute-start.2 = (f32[7,1,192,128]{3,1,2,0:T(1,128)S(1)}, f32[7,1,192,128]{3,1,2,0:T(1,128)}, u32[]{:S(2)}, u32[]{:S(2)}) collective-permute-start(f32[7,1,192,128]{3,1,2,0:T(1,128)S(1)} %get-tuple-element.30), channel_id=1, source_target_pairs={{0,1},{1,32},{32,33},{33,64},{64,65},{65,96},{96,97},{97,0},{2,3},... | collective-permute-start | bytes 2064392 | tf_op jit(solution)/shard_map/ppermute | solution.py:19
  181.7 26.8 %copy-start.11 = (f32[192]{0:T(256)S(1)}, f32[192]{0:T(256)}, u32[]{:S(2)}) copy-start(f32[192]{0:T(256)} %param.9) | copy-start | bytes 2308
  181.7 106.5 %collective-permute-start.3 = (f32[7,1,192,128]{3,1,2,0:T(1,128)S(1)}, f32[7,1,192,128]{3,1,2,0:T(1,128)}, u32[]{:S(2)}, u32[]{:S(2)}) collective-permute-start(f32[7,1,192,128]{3,1,2,0:T(1,128)S(1)} %get-tuple-element.31), channel_id=1, source_target_pairs={{1,0},{32,1},{33,32},{64,33},{65,64},{96,65},{97,96},{0,97},{3,2},... | collective-permute-start | bytes 2064392 | tf_op jit(solution)/shard_map/ppermute | solution.py:20
  264.1 8.9 %copy-start.8 = (f32[128]{0:T(128)S(1)}, f32[128]{0:T(128)}, u32[]{:S(2)}) copy-start(f32[128]{0:T(128)} %get-tuple-element.9) | copy-start | bytes 1540
  264.1 8.9 %copy-start.12 = (f32[128]{0:T(128)S(1)}, f32[128]{0:T(128)}, u32[]{:S(2)}) copy-start(f32[128]{0:T(128)} %param.10) | copy-start | bytes 1540
  273.0 21.2 %copy-start.9 = (f32[16]{0:T(128)S(1)}, f32[16]{0:T(128)}, u32[]{:S(2)}) copy-start(f32[16]{0:T(128)} %get-tuple-element.10) | copy-start | bytes 196
  273.0 21.2 %copy-start.10 = (f32[16]{0:T(128)S(1)}, f32[16]{0:T(128)}, u32[]{:S(2)}) copy-start(f32[16]{0:T(128)} %get-tuple-element.11) | copy-start | bytes 196
  273.0 21.2 %copy-start.13 = (f32[16]{0:T(128)S(1)}, f32[16]{0:T(128)}, u32[]{:S(2)}) copy-start(f32[16]{0:T(128)} %param.8) | copy-start | bytes 196
  332.0 20.6 %copy-start.1 = (f32[192,192]{1,0:T(8,128)S(1)}, f32[192,192]{1,0:T(8,128)}, u32[]{:S(2)}) copy-start(f32[192,192]{1,0:T(8,128)} %param.12) | copy-start | bytes 442372
where the time goes:
time: 357 us; the launch traced here: 353 us
  other arithmetic  149 us (42%)
  local copies, waits for them, and re-layouts  114 us (32%)
  matrix products  69 us (19%)
  starting transfers between devices  17 us (5%)
  between operations  3.77 us (1%)
    dot_general x3, matrix products, block_solve(): return jnp.einsum(form, inverse, source, precision=lax.Precision.HIGHEST)  69 us
    unnamed x47, local copies, waits for them, and re-layouts  38.4 us
    slice x4, local copies, waits for them, and re-layouts, pick(): return lax.slice_in_dim(values, position, position + 1, axis=axis_of)  28.3 us
    mul x3, other arithmetic, direction_fields(): velocity * velocity[direction:direction + 1]  18 us
    add x1, other arithmetic, on_device(): convection = result_x[3:] + result_y[3:] + result_z[3:]  17.4 us
    div x3, other arithmetic, combine_ends(): (left_value - COUPLING * left_tail * own_head) / (1.0 - COUPLING * COUPLI...  15.2 us
    mul x1, other arithmetic, on_device(): block_solve(stencil(wide_y, 2, count_y), y_inverse, 2)  14.5 us
    mul x1, other arithmetic, on_device(): combine_ends(inside_z, nearby_z, z_inverse, 3)  14 us
  transfers between devices with their start and end apart: 8, of which 0 were waited for; matrix products, arithmetic and copies ran while one was open for 50% of the time, Pallas kernels for 0%

commit v1 on v0

v1 whole, which is shorter than its diff:
```python
import functools

import jax
import jax.numpy as jnp
from jax import lax
from jax.experimental import pallas as pl
from jax.experimental.pallas import tpu as pltpu
from jax.sharding import PartitionSpec as P

COUPLING = 1.0 / 3.0
NEAR = 7.0 / 9.0
FAR = 1.0 / 36.0
F32 = jnp.float32
BF16 = jnp.bfloat16
MESH = pl.DeviceIdType.MESH
HIGH = lax.Precision.HIGHEST
CHUNKS = 2
MIB = 1 << 20


def split(values):
    high = values.astype(BF16)
    return high, (values - high.astype(F32)).astype(BF16)


def iota(shape, dim):
    return lax.broadcasted_iota(jnp.int32, shape, dim)


def band(size):
    step = iota((size, size), 1) - iota((size, size), 0)
    near = jnp.where(step == 1, NEAR, jnp.where(step == -1, -NEAR, 0.0))
    far = jnp.where(step == 2, FAR, jnp.where(step == -2, -FAR, 0.0))
    return (near + far).astype(F32)


def dot(a, b, dims=((1,), (0,)), precision=None):
    return lax.dot_general(a, b, (dims, ((), ())), precision=precision, preferred_element_type=F32)


def tap(row, j, size):
    def at(k):
        return row(k) if 0 <= k < size else None

    total = None
    for k, weight in ((j - 1, NEAR), (j + 1, -NEAR), (j - 2, FAR), (j + 2, -FAR)):
        value = at(k)
        if value is not None:
            total = weight * value if total is None else total + weight * value
    return total


def z_select(z_inverse, store):
    size = z_inverse.shape[0]
    local = dot(z_inverse, band(size), precision=HIGH)
    first, last = local[0:1], local[size - 1 : size]
    row, col = iota((32, size), 0), iota((32, size), 1)
    for field in range(6):
        rows = jnp.where(row == 16 + field, first, 0.0) + jnp.where(row == 24 + field, last, 0.0)
        if field < 3:
            for place, cell in ((field, 0), (3 + field, 1), (8 + field, size - 2), (11 + field, size - 1)):
                rows = jnp.where((row == place) & (col == cell), 1.0, rows)
        high, low = split(rows)
        both = jnp.concatenate([high, low], axis=0)
        store[field] = jnp.concatenate([both, both], axis=1)


def z_end_weights(z_inverse):
    size = z_inverse.shape[0]
    row, col = iota((16, 32), 0), iota((16, 32), 1)
    weights = jnp.zeros((16, 32), F32)
    for end, line in ((0, 0), (8, size - 1)):
        ends = [z_inverse[line : line + 1, k : k + 1] for k in (0, 1, size - 2, size - 1)]
        terms = (
            (0, -FAR * ends[0]),
            (3, -NEAR * ends[0] - FAR * ends[1]),
            (16, NEAR * ends[3] + FAR * ends[2]),
            (19, FAR * ends[3]),
        )
        for field in range(6):
            base = field % 3 + (0 if field < 3 else 8)
            for place, value in terms:
                weights = jnp.where((row == end + field) & (col == base + place), value, weights)
    return weights


def exchange_kernel(
    v_hbm, x_inv, z_inv,
    z_rows, xh, xp, xe, xc,
    vv, sel, zs1, zs2, zh, zp, xcs, wtab,
    load_sem, x1s, x1r, x2s, x2r, z1s, z1r, z2s, z2r, xcsem, xcrecv,
):
    gx, gy, gz = lax.axis_index("gx"), lax.axis_index("gy"), lax.axis_index("gz")
    nx, ny, nz = lax.axis_size("gx"), lax.axis_size("gy"), lax.axis_size("gz")
    me = gx * ny + gy
    count = nx * ny
    xl, xr = lax.rem(me + count - 1, count), lax.rem(me + 1, count)
    left = {"gx": xl // ny, "gy": lax.rem(xl, ny)}
    right = {"gx": xr // ny, "gy": lax.rem(xr, ny)}
    below = {"gz": lax.rem(gz + nz - 1, nz)}
    above = {"gz": lax.rem(gz + 1, nz)}
    barrier = pltpu.get_barrier_semaphore()
    for device in (left, right, below, above):
        pl.semaphore_signal(barrier, inc=1, device_id=device, device_id_type=MESH)

    cx, rows, cz = vv.shape[1:]
    loads = [pltpu.make_async_copy(v_hbm.at[i], vv.at[i], load_sem.at[i]) for i in range(3)]
    for load in loads:
        load.start()
    tile = (8, 128)
    xcs[0] = jnp.full(tile, x_inv[0, 0], F32)
    xcs[1] = jnp.full(tile, x_inv[cx - 1, cx - 1], F32)
    for end, line in ((0, 0), (1, cx - 1)):
        for j in range(-2, cx + 2):
            wtab[end * (cx + 4) + j + 2] = jnp.full(tile, tap(lambda k: x_inv[line, k], j, cx), F32)
    pl.semaphore_wait(barrier, 4)

    def send(src, dst, s, r, device):
        return pltpu.make_async_remote_copy(
            src_ref=src, dst_ref=dst, send_sem=s, recv_sem=r, device_id=device, device_id_type=MESH)

    step = rows // CHUNKS
    faces = []
    for c in range(CHUNKS):
        part = pl.ds(c * step, step)
        pair = (
            send(v_hbm.at[:, pl.ds(cx - 2, 2), part], xh.at[0, :, :, part], x1s.at[0, c], x1r.at[0, c], right),
            send(v_hbm.at[:, pl.ds(0, 2), part], xh.at[1, :, :, part], x1s.at[1, c], x1r.at[1, c], left),
        )
        for copy in pair:
            copy.start()
        faces.append(pair)
    corners = (
        send(xcs.at[1], xc.at[0], xcsem.at[0], xcrecv.at[0], right),
        send(xcs.at[0], xc.at[1], xcsem.at[1], xcrecv.at[1], left),
    )
    for copy in corners:
        copy.start()

    zi = z_inv[...]
    z_select(zi, sel)
    size = zi.shape[0]
    corner = (zi[0:1, 0:1], zi[size - 1 : size, size - 1 : size])
    for load in loads:
        load.wait()

    @pl.loop(0, cx)
    def _(x):
        v = [vv[i, x] for i in range(3)]
        total = jnp.zeros((64, rows), F32)
        for field in range(6):
            value = v[field] if field < 3 else v[field - 3] * v[2]
            total = total + dot(sel[field], jnp.concatenate(split(value), axis=1), ((1,), (1,)))
        got = total[0:32] + total[32:64]
        spare = iota((8, rows), 0) == 6
        zs1[0, x] = jnp.where(spare, corner[0], got[0:8])
        zs1[1, x] = jnp.where(spare, corner[1], got[8:16])
        zs2[0, x] = got[16:24]
        zs2[1, x] = got[24:32]

    z_faces = (
        send(zs1.at[1], zh.at[0], z1s.at[0], z1r.at[0], above),
        send(zs1.at[0], zh.at[1], z1s.at[1], z1r.at[1], below),
    )
    for copy in z_faces:
        copy.start()

    @pl.loop(0, rows // 8)
    def _(t):
        part = pl.ds(pl.multiple_of(t * 8, 8), 8)
        ends = [[None] * 6, [None] * 6]
        for j in range(cx):
            v = [vv[i, j, part] for i in range(3)]
            fields = v + [a * v[0] for a in v]
            for end in range(2):
                weight = wtab[end * (cx + 4) + j + 2]
                for f in range(6):
                    term = weight * fields[f]
                    ends[end][f] = term if ends[end][f] is None else ends[end][f] + term
        for end in range(2):
            for f in range(6):
                xe[end, f, part] = ends[end][f]

    for copy in z_faces:
        copy.wait()
    wz = split(z_end_weights(zi))
    wz = jnp.concatenate([wz[0], wz[0], wz[1]], axis=1)

    @pl.loop(0, cx)
    def _(x):
        row = iota((8, rows), 0)
        halo = []
        for side in range(2):
            h = zh[side, x]
            halo += [h, h * jnp.where(row < 3, h[2:3], h[5:6])]
        halo = jnp.concatenate(halo, axis=0)
        high, low = split(halo)
        more = dot(wz, jnp.concatenate([high, low, high], axis=0))
        z_rows[x, 0:32] = halo
        first = zs2[0, x] + more[0:8]
        last = zs2[1, x] + more[8:16]
        zs2[0, x] = first
        zs2[1, x] = last
        z_rows[x, 48:56] = first
        z_rows[x, 56:64] = last

    z_ends = (
        send(zs2.at[1], zp.at[0], z2s.at[0], z2r.at[0], above),
        send(zs2.at[0], zp.at[1], z2s.at[1], z2r.at[1], below),
    )
    for copy in z_ends:
        copy.start()

    x_ends = []
    for c in range(CHUNKS):
        for copy in faces[c]:
            copy.wait()

        @pl.loop(0, step // 8)
        def _(t):
            part = pl.ds(pl.multiple_of(c * step + t * 8, 8), 8)
            ends = [[xe[end, f, part] for f in range(6)] for end in range(2)]
            for side in range(2):
                for layer in range(2):
                    j = layer - 2 if side == 0 else cx + layer
                    v = [xh[side, i, layer, part] for i in range(3)]
                    fields = v + [a * v[0] for a in v]
                    for end in range(2):
                        weight = wtab[end * (cx + 4) + j + 2]
                        for f in range(6):
                            ends[end][f] = ends[end][f] + weight * fields[f]
            for end in range(2):
                for f in range(6):
                    xe[end, f, part] = ends[end][f]

        part = pl.ds(c * step, step)
        pair = (
            send(xe.at[1, :, part], xp.at[0, :, part], x2s.at[0, c], x2r.at[0, c], right),
            send(xe.at[0, :, part], xp.at[1, :, part], x2s.at[1, c], x2r.at[1, c], left),
        )
        for copy in pair:
            copy.start()
        x_ends.append(pair)

    for copy in z_ends:
        copy.wait()
    for side in range(2):
        z_rows[:, 32 + 8 * side : 40 + 8 * side] = zp[side]
    for copy in corners:
        copy.wait()
    for pair in x_ends:
        for copy in pair:
            copy.wait()


def exchange(velocity, x_inverse, z_inverse):
    _, cx, rows, cz = velocity.shape
    vmem = pl.BlockSpec(memory_space=pltpu.VMEM)
    dma = pltpu.SemaphoreType.DMA
    return pl.pallas_call(
        exchange_kernel,
        out_shape=(
            jax.ShapeDtypeStruct((cx, 64, rows), F32),
            jax.ShapeDtypeStruct((2, 3, 2, rows, cz), F32),
            jax.ShapeDtypeStruct((2, 6, rows, cz), F32),
            jax.ShapeDtypeStruct((2, 6, rows, cz), F32),
            jax.ShapeDtypeStruct((2, 8, 128), F32),
        ),
        in_specs=[
            pl.BlockSpec(memory_space=pl.ANY),
            pl.BlockSpec(memory_space=pltpu.SMEM),
            vmem,
        ],
        out_specs=(vmem,) * 5,
        scratch_shapes=[
            pltpu.VMEM((3, cx, rows, cz), F32),
            pltpu.VMEM((6, 64, 2 * cz), BF16),
            pltpu.VMEM((2, cx, 8, rows), F32),
            pltpu.VMEM((2, cx, 8, rows), F32),
            pltpu.VMEM((2, cx, 8, rows), F32),
            pltpu.VMEM((2, cx, 8, rows), F32),
            pltpu.VMEM((2, 8, 128), F32),
            pltpu.VMEM((2 * (cx + 4), 8, 128), F32),
            dma((3,)),
            dma((2, CHUNKS)), dma((2, CHUNKS)), dma((2, CHUNKS)), dma((2, CHUNKS)),
            dma((2,)), dma((2,)), dma((2,)), dma((2,)), dma((2,)), dma((2,)),
        ],
        compiler_params=pltpu.CompilerParams(
            collective_id=0, has_side_effects=True, vmem_limit_bytes=20 * MIB),
        name="exchange",
    )(velocity, x_inverse, z_inverse)


def z_tables(z_inverse, metric, tail_left, first_right, weights, spread):
    size = z_inverse.shape[0]
    local = dot(z_inverse, band(size), precision=HIGH)
    high, low = split(local.T * metric)
    both = jnp.concatenate([high, low], axis=1)
    weights[...] = jnp.concatenate([both, both], axis=0)
    columns = z_inverse.T
    c0, c1 = columns[0:1] * metric, columns[1:2] * metric
    c2, c3 = columns[size - 2 : size - 1] * metric, columns[size - 1 : size] * metric
    own_first, own_last = columns[0:1, 0:1], columns[size - 1 : size, size - 1 : size]
    scale_left = COUPLING / (1.0 - COUPLING * COUPLING * tail_left * own_first)
    scale_right = COUPLING / (1.0 - COUPLING * COUPLING * own_last * first_right)
    row = iota((64, size), 0)
    for field in range(6):
        base = field % 3 + (0 if field < 3 else 8)
        terms = (
            (base, -FAR * c0),
            (base + 3, -NEAR * c0 - FAR * c1),
            (base + 16, NEAR * c3 + FAR * c2),
            (base + 19, FAR * c3),
            (32 + field, -scale_left * c0),
            (40 + field, -scale_right * c3),
            (48 + field, COUPLING * tail_left * scale_left * c0),
            (56 + field, COUPLING * first_right * scale_right * c3),
        )
        table = jnp.zeros((64, size), F32)
        for place, value in terms:
            table = jnp.where(row == place, value, table)
        high, low = split(table)
        spread[:, field * size : (field + 1) * size] = jnp.concatenate([high, high, low], axis=0)


def y_table(y_inverse, metric):
    size = y_inverse.shape[0]
    own = iota((size, size), 0) == iota((size, size), 1)
    column = jnp.sum(jnp.where(own, metric, 0.0), axis=1, keepdims=True)
    high, low = split(dot(y_inverse, band(size), precision=HIGH) * column)
    return jnp.concatenate([high, high, low], axis=1)


def yz_kernel(v_ref, rows_ref, yi, my, zi, mz, corner, grad, conv, ytab, ztab, spread):
    @pl.when(pl.program_id(0) == 0)
    def _():
        ytab[...] = y_table(yi[...], my[...])
        z_tables(zi[...], mz[...], corner[0, 6:7, 0:1], corner[1, 6:7, 0:1], ztab, spread)

    pair, rows, cz = v_ref.shape[1:]
    v = [[v_ref[i, x] for x in range(pair)] for i in range(3)]
    parts = [[split(v[i][x]) for x in range(pair)] for i in range(3)]

    def along_y(piece):
        high = jnp.concatenate([p[0] for p in piece], axis=1)
        low = jnp.concatenate([p[1] for p in piece], axis=1)
        return dot(ytab[...], jnp.concatenate([high, low, high], axis=0))

    def along_z(piece, x, field):
        got = dot(jnp.concatenate(piece, axis=1), ztab[...])
        return got[:, :cz] + got[:, cz:]

    extra = []
    for x in range(pair):
        high, low = split(rows_ref[x])
        extra.append(dot(jnp.concatenate([high, low, high], axis=0), spread[...], ((0,), (0,))))
    for i in range(3):
        got = along_y(parts[i])
        for x in range(pair):
            grad[0, i, x] = got[:, x * cz : (x + 1) * cz]
        got = along_y([split(v[i][x] * v[1][x]) for x in range(pair)])
        for x in range(pair):
            grad[1, i, x] = along_z(parts[i][x], x, i) + extra[x][:, i * cz : (i + 1) * cz]
            second = along_z(split(v[i][x] * v[2][x]), x, 3 + i)
            conv[i, x] = got[:, x * cz : (x + 1) * cz] + (second + extra[x][:, (3 + i) * cz : (4 + i) * cz])


def yz(velocity, z_rows, y_inverse, metric_y, z_inverse, metric_z):
    _, cx, rows, cz = velocity.shape
    pair = 2
    return pl.pallas_call(
        yz_kernel,
        grid=(cx // pair,),
        out_shape=(
            jax.ShapeDtypeStruct((2, 3, cx, rows, cz), F32),
            jax.ShapeDtypeStruct((3, cx, rows, cz), F32),
        ),
        in_specs=[
            pl.BlockSpec((3, pair, rows, cz), lambda x: (0, x, 0, 0)),
            pl.BlockSpec((pair, 64, rows), lambda x: (x, 0, 0)),
            pl.BlockSpec((rows, rows), lambda x: (0, 0)),
            pl.BlockSpec((1, rows), lambda x: (0, 0)),
            pl.BlockSpec((cz, cz), lambda x: (0, 0)),
            pl.BlockSpec((1, cz), lambda x: (0, 0)),
            pl.BlockSpec((2, 8, 128), lambda x: (0, 0, 0)),
        ],
        out_specs=(
            pl.BlockSpec((2, 3, pair, rows, cz), lambda x: (0, 0, x, 0, 0)),
            pl.BlockSpec((3, pair, rows, cz), lambda x: (0, x, 0, 0)),
        ),
        scratch_shapes=[
            pltpu.VMEM((rows, 3 * rows), BF16),
            pltpu.VMEM((2 * cz, 2 * cz), BF16),
            pltpu.VMEM((192, 6 * cz), BF16),
        ],
        compiler_params=pltpu.CompilerParams(vmem_limit_bytes=20 * MIB),
        name="yz",
    )(velocity, z_rows, y_inverse, metric_y.reshape(1, rows), z_inverse, metric_z.reshape(1, cz),
      jnp.stack([z_rows[0, 0:8, 0:128], z_rows[0, 16:24, 0:128]]))


def x_kernel(v_ref, xh, xp, xe, xc, x_inv, mx, gyz, cyz, grad, conv, tab):
    cx = v_ref.shape[1]
    tile = (8, 128)

    @pl.when(pl.program_id(0) == 0)
    def _():
        def full(value):
            return jnp.full(tile, value, F32)

        def inv(i, j):
            return full(x_inv[i, j])

        before = None
        for i in range(cx):
            metric = full(mx[i])
            if i < cx - 1:
                up = inv(i, i + 1) / inv(i + 1, i + 1)
                own = inv(i, i) - up * inv(i + 1, i)
                tab[2 * cx + i] = up * metric / full(mx[i + 1])
            else:
                own = inv(i, i)
            if i > 0:
                down = inv(i, i - 1)
                if i < cx - 1:
                    down = down - up * inv(i + 1, i - 1)
                tab[cx + i] = down / before * metric / full(mx[i - 1])
            tab[i] = NEAR * metric * own
            before = own
        square = COUPLING * COUPLING
        for side, corner in ((0, inv(0, 0)), (1, inv(cx - 1, cx - 1))):
            other = xc[side]
            scale = (COUPLING / NEAR) / (1.0 - square * other * corner)
            tab[3 * cx + 2 * side] = scale
            tab[3 * cx + 2 * side + 1] = COUPLING * other * scale

    @pl.loop(0, v_ref.shape[2] // 8)
    def _(t):
        part = pl.ds(pl.multiple_of(t * 8, 8), 8)

        def cell(j):
            if j < 0:
                v = [xh[0, i, j + 2, part] for i in range(3)]
            elif j >= cx:
                v = [xh[1, i, j - cx, part] for i in range(3)]
            else:
                v = [v_ref[i, j, part] for i in range(3)]
            return v + [a * v[0] for a in v]

        window = [cell(j) for j in range(-2, 2)]
        state = None
        for j in range(cx):
            window.append(cell(j + 2))
            fresh = []
            for f in range(6):
                d = (window[3][f] - window[1][f]) + (FAR / NEAR) * (window[4][f] - window[0][f])
                for side, line in ((0, 0), (1, cx - 1)):
                    if j == line:
                        k = 3 * cx + 2 * side
                        d = d - tab[k] * xp[side, f, part] + tab[k + 1] * xe[side, f, part]
                value = tab[j] * d
                if state is not None:
                    value = value + tab[cx + j] * state[f]
                fresh.append(value)
                if j < cx - 1:
                    if f < 3:
                        grad[f, 0, j, part] = value
                    else:
                        conv[f - 3, j, part] = value
            state = fresh
            window.pop(0)
        for j in range(cx - 1, -1, -1):
            if j < cx - 1:
                up = tab[2 * cx + j]
                state = [
                    (grad[f, 0, j, part] if f < 3 else conv[f - 3, j, part]) + up * state[f]
                    for f in range(6)
                ]
            for i in range(3):
                grad[i, 0, j, part] = state[i]
                grad[i, 1, j, part] = gyz[0, i, j, part]
                grad[i, 2, j, part] = gyz[1, i, j, part]
                conv[i, j, part] = state[3 + i] + cyz[i, j, part]


def x_solve(velocity, xh, xp, xe, xc, x_inverse, metric_x, gyz, cyz):
    _, cx, rows, cz = velocity.shape
    step = 16
    smem = pl.BlockSpec(memory_space=pltpu.SMEM)
    return pl.pallas_call(
        x_kernel,
        grid=(rows // step,),
        out_shape=(
            jax.ShapeDtypeStruct((3, 3, cx, rows, cz), F32),
            jax.ShapeDtypeStruct((3, cx, rows, cz), F32),
        ),
        in_specs=[
            pl.BlockSpec((3, cx, step, cz), lambda y: (0, 0, y, 0)),
            pl.BlockSpec((2, 3, 2, step, cz), lambda y: (0, 0, 0, y, 0)),
            pl.BlockSpec((2, 6, step, cz), lambda y: (0, 0, y, 0)),
            pl.BlockSpec((2, 6, step, cz), lambda y: (0, 0, y, 0)),
            pl.BlockSpec((2, 8, 128), lambda y: (0, 0, 0)),
            smem,
            smem,
            pl.BlockSpec((2, 3, cx, step, cz), lambda y: (0, 0, 0, y, 0)),
            pl.BlockSpec((3, cx, step, cz), lambda y: (0, 0, y, 0)),
        ],
        out_specs=(
            pl.BlockSpec((3, 3, cx, step, cz), lambda y: (0, 0, 0, y, 0)),
            pl.BlockSpec((3, cx, step, cz), lambda y: (0, 0, y, 0)),
        ),
        scratch_shapes=[pltpu.VMEM((3 * cx + 4, 8, 128), F32)],
        compiler_params=pltpu.CompilerParams(vmem_limit_bytes=20 * MIB),
        name="x_solve",
    )(velocity, xh, xp, xe, xc, x_inverse, metric_x, gyz, cyz)


def on_device(velocity, metric_x, metric_y, metric_z, x_inverse, y_inverse, z_inverse):
    z_rows, xh, xp, xe, xc = exchange(velocity, x_inverse, z_inverse)
    gyz, cyz = yz(velocity, z_rows, y_inverse, metric_y, z_inverse, metric_z)
    return tuple(x_solve(velocity, xh, xp, xe, xc, x_inverse, metric_x, gyz, cyz))


def solution(mesh):
    return jax.shard_map(
        on_device,
        mesh=mesh,
        in_specs=(
            P(None, ("gx", "gy"), None, "gz"),
            P(("gx", "gy")),
            P(),
            P("gz"),
            P(("gx", "gy"), None),
            P(),
            P("gz", None),
        ),
        out_specs=(P(None, None, ("gx", "gy"), None, "gz"), P(None, ("gx", "gy"), None, "gz")),
        check_vma=False,
    )
```

time: 357 us -> 56.7 us (0.16)
  other arithmetic: 149 us -> 0.01 us
  local copies, waits for them, and re-layouts: 114 us -> 3.9 us
  matrix products: 69 us -> 0 us
  Pallas kernels: 0 us -> 51 us
  starting transfers between devices: 17 us -> 0 us
    dot_general x3 -> x0, matrix products: 69 us -> none  [block_solve(): return jnp.einsum(form, inverse, source, precision=lax.Precision.HIGHEST)]
    mul x10 -> x0, other arithmetic: 59.4 us -> none  [the longest x3 18 us: direction_fields(): velocity * velocity[direction:direction + 1]]
    pallas_call x0 -> x3, Pallas kernels: none -> 51 us  [the longest x1 29.1 us: exchange(): pl.pallas_call(exchange_kernel, out_shape=(jax.ShapeDtypeStruct((cx, 64,...]
    slice x10 -> x1, local copies, waits for them, and re-layouts: 42.6 us -> 0.01 us  [yz(): z_rows[0, 0:8, 0:128]]
    unnamed x47 -> x16, local copies, waits for them, and re-layouts: 38.4 us -> 3.9 us
    add x2 -> x0, other arithmetic: 31 us -> none  [the longest x1 17.4 us: on_device(): convection = result_x[3:] + result_y[3:] + result_z[3:]]
    div x5 -> x0, other arithmetic: 25.3 us -> none  [the longest x3 15.2 us: combine_ends(): (left_value - COUPLING * left_tail * own_head) / (1.0 - COUPLING * COUPLI...]
    mul x5 -> x0, local copies, waits for them, and re-layouts: 21 us -> none  [the longest x1 8.92 us: combine_ends(): COUPLING * column_first * left_final]
  transfers between devices with their start and end apart: 8 -> 0, of which waited for: 0 -> 0; matrix products, arithmetic and copies ran while one was open for 50% -> 0% of each run, Pallas kernels for 0% -> 0%
where the time goes in v1:
time: 56.7 us; the launch traced here: 55.6 us
  Pallas kernels  51 us (90%)
  local copies, waits for them, and re-layouts  3.9 us (7%)
  between operations  0.73 us (1%)
    pallas_call x1, Pallas kernels, exchange(): pl.pallas_call(exchange_kernel, out_shape=(jax.ShapeDtypeStruct((cx, 64,...  29.1 us
    pallas_call x1, Pallas kernels, yz(): pl.pallas_call(yz_kernel, grid=(cx // pair,), out_shape=(jax.ShapeDtypeSt...  11 us
    pallas_call x1, Pallas kernels, x_solve(): pl.pallas_call(x_kernel, grid=(rows // step,), out_shape=(jax.ShapeDtypeS...  10.9 us
    unnamed x16, local copies, waits for them, and re-layouts  3.9 us

profile of v1, /device:TPU:0, one launch (start us, length us, event | category | flops | bytes accessed | tf_op | source)
XLA Modules:
  0.0 55.6 jit_solution(16968508211335548971)
XLA Ops:
  0.6 0.0 copy-start.7
  0.6 0.0 copy-start.5
  0.7 0.0 copy-start
  0.7 2.3 %copy-done = f32[3,16,192,128]{3,2,1,0:T(8,128)S(1)} copy-done((f32[3,16,192,128]{3,2,1,0:T(8,128)S(1)}, f32[3,16,192,128]{3,2,1,0:T(8,128)}, u32[]{:S(2)}) %copy-start) | copy-done | bytes 4718616
  3.0 0.0 copy-start.1
  3.0 0.8 %copy-done.1 = f32[128,128]{1,0:T(8,128)S(1)} copy-done((f32[128,128]{1,0:T(8,128)S(1)}, f32[128,128]{1,0:T(8,128)}, u32[]{:S(2)}) %copy-start.1) | copy-done | bytes 65560
  3.8 0.0 copy-start.4
  3.8 0.7 %copy-done.4 = f32[16,16]{1,0:T(8,128)S(1)} copy-done((f32[16,16]{1,0:T(8,128)S(1)}, f32[16,16]{1,0:T(8,128)}, u32[]{:S(2)}) %copy-start.4) | copy-done | bytes 1048
  4.5 0.0 copy-start.2
  4.5 0.0 copy-start.3
  4.5 0.0 copy-start.6
  4.5 29.1 %exchange.1 = (f32[16,64,192]{2,1,0:T(8,128)S(1)}, f32[2,3,2,192,128]{4,3,2,1,0:T(8,128)S(1)}, f32[2,6,192,128]{3,2,1,0:T(8,128)S(1)}, f32[2,6,192,128]{3,2,1,0:T(8,128)S(1)}, f32[2,8,128]{2,1,0:T(8,128)S(1)}) custom-call(f32[3,16,192,128]{3,2,1,0:T(8,128)S(1)} %copy-done, f32[16,16]{1,0:T(8,128)S(1)} %copy-done.4, f32[128,128]{1,0:T(8,128)S(1)} %copy-done.1), custom_call_target="tpu_custom_call" | custom-call | tf_op jit(solution)/shard_map/exchange/pallas_call | solution.py:260
  33.6 0.0 copy-done.7
  33.7 0.0 copy-done.5
  33.7 0.0 copy-done.2
  33.7 0.0 copy-done.3
  33.7 11.0 %yz.1 = (f32[2,3,16,192,128]{4,3,2,1,0:T(8,128)S(1)}, f32[3,16,192,128]{3,2,1,0:T(8,128)S(1)}) custom-call(f32[3,16,192,128]{3,2,1,0:T(8,128)S(1)} %copy-done, f32[16,64,192]{2,1,0:T(8,128)S(1)} %get-tuple-element.13.rows_ref, f32[192,192]{1,0:T(8,128)S(1)} %copy-done.3, f32[1,192]{1,0:T(1,128)S(1)} %bitcast.2, f32[128,128]{1,0:T(8,128)S(1)} %copy-done.2, ...), custom_call_target="tpu_custom_call" | custom-call | tf_op jit(solution)/shard_map/yz/pallas_call | solution.py:371
  44.7 0.0 copy-done.6
  44.8 10.9 %x_solve.1 = (f32[3,3,16,192,128]{4,3,2,1,0:T(8,128)}, f32[3,16,192,128]{3,2,1,0:T(8,128)}) custom-call(f32[3,16,192,128]{3,2,1,0:T(8,128)S(1)} %copy-done, f32[2,3,2,192,128]{4,3,2,1,0:T(8,128)S(1)} %get-tuple-element.9.xh, f32[2,6,192,128]{3,2,1,0:T(8,128)S(1)} %get-tuple-element.10.xp, f32[2,6,192,128]{3,2,1,0:T(8,128)S(1)} %get-tuple-element.11.xe, ...), custom_call_target="tpu_custom_call" | custom-call | tf_op jit(solution)/shard_map/x_solve/pallas_call | solution.py:490
  (2 shorter events, 0.0 us)
Async XLA Ops:
  0.6 33.0 %copy-start.7 = (f32[128]{0:T(128)S(1)}, f32[128]{0:T(128)}, u32[]{:S(2)}) copy-start(f32[128]{0:T(128)} %param.10) | copy-start | bytes 1540
  0.6 33.0 %copy-start.5 = (f32[192]{0:T(256)S(1)}, f32[192]{0:T(256)}, u32[]{:S(2)}) copy-start(f32[192]{0:T(256)} %param.9) | copy-start | bytes 2308
  0.7 2.3 %copy-start = (f32[3,16,192,128]{3,2,1,0:T(8,128)S(1)}, f32[3,16,192,128]{3,2,1,0:T(8,128)}, u32[]{:S(2)}) copy-start(f32[3,16,192,128]{3,2,1,0:T(8,128)} %v_ref.3) | copy-start | bytes 14155780
  3.0 0.8 %copy-start.1 = (f32[128,128]{1,0:T(8,128)S(1)}, f32[128,128]{1,0:T(8,128)}, u32[]{:S(2)}) copy-start(f32[128,128]{1,0:T(8,128)} %zi.1) | copy-start | bytes 196612
  3.8 0.7 %copy-start.4 = (f32[16,16]{1,0:T(8,128)S(1)}, f32[16,16]{1,0:T(8,128)}, u32[]{:S(2)}) copy-start(f32[16,16]{1,0:T(8,128)} %x_inv.3) | copy-start | bytes 3076
  4.5 29.1 %copy-start.2 = (f32[128,128]{1,0:T(8,128)S(1)}, f32[128,128]{1,0:T(8,128)}, u32[]{:S(2)}) copy-start(f32[128,128]{1,0:T(8,128)} %zi.1) | copy-start | bytes 196612
  4.5 29.1 %copy-start.3 = (f32[192,192]{1,0:T(8,128)S(1)}, f32[192,192]{1,0:T(8,128)}, u32[]{:S(2)}) copy-start(f32[192,192]{1,0:T(8,128)} %yi.1) | copy-start | bytes 442372
  4.5 40.2 %copy-start.6 = (f32[16]{0:T(128)S(1)}, f32[16]{0:T(128)}, u32[]{:S(2)}) copy-start(f32[16]{0:T(128)} %mx.1) | copy-start | bytes 196

commit v2 on v0

v2 whole, which is shorter than its diff:
```python
import jax
import jax.numpy as jnp
from jax import lax
from jax.experimental import pallas as pl
from jax.experimental.pallas import tpu as pltpu
from jax.sharding import PartitionSpec as P

COUPLING = 1.0 / 3.0
NEAR = 7.0 / 9.0
FAR = 1.0 / 36.0
F32 = jnp.float32
BF16 = jnp.bfloat16
MESH = pl.DeviceIdType.MESH
HIGH = lax.Precision.HIGHEST
CHUNKS = 2
BETWEEN = 1
OUT_CHUNKS = 6
MIB = 1 << 20


def split(values):
    high = values.astype(BF16)
    return high, (values - high.astype(F32)).astype(BF16)


def iota(shape, dim):
    return lax.broadcasted_iota(jnp.int32, shape, dim)


def band(size):
    step = iota((size, size), 1) - iota((size, size), 0)
    near = jnp.where(step == 1, NEAR, jnp.where(step == -1, -NEAR, 0.0))
    far = jnp.where(step == 2, FAR, jnp.where(step == -2, -FAR, 0.0))
    return (near + far).astype(F32)


def dot(a, b, dims=((1,), (0,)), precision=None):
    return lax.dot_general(a, b, (dims, ((), ())), precision=precision, preferred_element_type=F32)


def tap(line, j):
    size = line.shape[1]
    total = jnp.zeros((1, 1), F32)
    for k, weight in ((j - 1, NEAR), (j + 1, -NEAR), (j - 2, FAR), (j + 2, -FAR)):
        if 0 <= k < size:
            total = total + weight * line[:, k : k + 1]
    return total


def full(value):
    return jnp.broadcast_to(value, (8, 128))


def z_select(z_inverse, store):
    size = z_inverse.shape[0]
    local = dot(z_inverse, band(size), precision=HIGH)
    first, last = local[0:1], local[size - 1 : size]
    row, col = iota((32, size), 0), iota((32, size), 1)
    for field in range(6):
        rows = jnp.where(row == 16 + field, first, 0.0) + jnp.where(row == 24 + field, last, 0.0)
        if field < 3:
            for place, cell in ((field, 0), (3 + field, 1), (8 + field, size - 2), (11 + field, size - 1)):
                rows = jnp.where((row == place) & (col == cell), 1.0, rows)
        high, low = split(rows)
        both = jnp.concatenate([high, low], axis=0)
        store[field] = jnp.concatenate([both, both], axis=1)


def z_end_weights(z_inverse):
    size = z_inverse.shape[0]
    row, col = iota((16, 32), 0), iota((16, 32), 1)
    weights = jnp.zeros((16, 32), F32)
    for end, line in ((0, 0), (8, size - 1)):
        ends = [z_inverse[line : line + 1, k : k + 1] for k in (0, 1, size - 2, size - 1)]
        terms = (
            (0, -FAR * ends[0]),
            (3, -NEAR * ends[0] - FAR * ends[1]),
            (16, NEAR * ends[3] + FAR * ends[2]),
            (19, FAR * ends[3]),
        )
        for field in range(6):
            base = field % 3 + (0 if field < 3 else 8)
            for place, value in terms:
                weights = jnp.where((row == end + field) & (col == base + place), value, weights)
    return weights


def z_tables(z_inverse, metric, tail_left, first_right, weights, spread):
    size = z_inverse.shape[0]
    local = dot(z_inverse, band(size), precision=HIGH)
    high, low = split(local.T * metric)
    both = jnp.concatenate([high, low], axis=1)
    weights[...] = jnp.concatenate([both, both], axis=0)
    columns = z_inverse.T
    c0, c1 = columns[0:1] * metric, columns[1:2] * metric
    c2, c3 = columns[size - 2 : size - 1] * metric, columns[size - 1 : size] * metric
    own_first, own_last = columns[0:1, 0:1], columns[size - 1 : size, size - 1 : size]
    scale_left = COUPLING / (1.0 - COUPLING * COUPLING * tail_left * own_first)
    scale_right = COUPLING / (1.0 - COUPLING * COUPLING * own_last * first_right)
    row = iota((64, size), 0)
    for field in range(6):
        base = field % 3 + (0 if field < 3 else 8)
        terms = (
            (base, -FAR * c0),
            (base + 3, -NEAR * c0 - FAR * c1),
            (base + 16, NEAR * c3 + FAR * c2),
            (base + 19, FAR * c3),
            (32 + field, -scale_left * c0),
            (40 + field, -scale_right * c3),
            (48 + field, COUPLING * tail_left * scale_left * c0),
            (56 + field, COUPLING * first_right * scale_right * c3),
        )
        table = jnp.zeros((64, size), F32)
        for place, value in terms:
            table = jnp.where(row == place, value, table)
        high, low = split(table)
        spread[:, field * size : (field + 1) * size] = jnp.concatenate([high, high, low], axis=0)


def y_table(y_inverse, metric):
    size = y_inverse.shape[0]
    own = iota((size, size), 0) == iota((size, size), 1)
    column = jnp.sum(jnp.where(own, metric, 0.0), axis=1, keepdims=True)
    high, low = split(dot(y_inverse, band(size), precision=HIGH) * column)
    return jnp.concatenate([high, high, low], axis=1)


def x_end_weights(inverse, store):
    size = inverse.shape[0]
    for end, line in ((0, 0), (1, size - 1)):
        for j in range(-2, size + 2):
            store[end * (size + 4) + j + 2] = full(tap(inverse[line : line + 1], j))


def x_tables(inverse, metric, corners, tab):
    size = inverse.shape[0]

    def inv(i, j):
        return inverse[i : i + 1, j : j + 1]

    before = None
    for i in range(size):
        scale = metric[:, i : i + 1]
        if i < size - 1:
            up = inv(i, i + 1) / inv(i + 1, i + 1)
            own = inv(i, i) - up * inv(i + 1, i)
            tab[2 * size + i] = full(up * scale / metric[:, i + 1 : i + 2])
        else:
            own = inv(i, i)
        if i > 0:
            down = inv(i, i - 1)
            if i < size - 1:
                down = down - up * inv(i + 1, i - 1)
            tab[size + i] = full(down / before * scale / metric[:, i - 1 : i])
        tab[i] = full(NEAR * scale * own)
        before = own
    for side, corner in ((0, inv(0, 0)), (1, inv(size - 1, size - 1))):
        other = corners[side]
        scale = (COUPLING / NEAR) / (1.0 - COUPLING * COUPLING * other * full(corner))
        tab[3 * size + 2 * side] = scale
        tab[3 * size + 2 * side + 1] = COUPLING * other * scale


def z_local(x, v, sel, corner, parts, zs1, zs2):
    rows = v.shape[2]
    velocity = [v[i, x] for i in range(3)]
    total = jnp.zeros((64, rows), F32)
    for field in range(6):
        value = velocity[field] if field < 3 else velocity[field - 3] * velocity[2]
        piece = jnp.concatenate(split(value), axis=1)
        parts[field, x] = piece
        total = total + dot(sel[field], piece, ((1,), (1,)))
    got = total[0:32] + total[32:64]
    spare = iota((8, rows), 0) == 6
    zs1[0, x] = jnp.where(spare, corner[0], got[0:8])
    zs1[1, x] = jnp.where(spare, corner[1], got[8:16])
    zs2[0, x] = got[16:24]
    zs2[1, x] = got[24:32]


def z_halo(x, zh, wz, z_rows, zs2):
    rows = zh.shape[3]
    row = iota((8, rows), 0)
    halo = []
    for side in range(2):
        h = zh[side, x]
        halo += [h, h * jnp.where(row < 3, h[2:3], h[5:6])]
    halo = jnp.concatenate(halo, axis=0)
    high, low = split(halo)
    more = dot(wz, jnp.concatenate([high, low, high], axis=0))
    z_rows[x, 0:32] = halo
    first = zs2[0, x] + more[0:8]
    last = zs2[1, x] + more[8:16]
    zs2[0, x] = first
    zs2[1, x] = last
    z_rows[x, 48:56] = first
    z_rows[x, 56:64] = last


def x_local(t, v, wtab, xe):
    part = pl.ds(pl.multiple_of(t * 8, 8), 8)
    size = v.shape[1]
    ends = [[None] * 6, [None] * 6]
    for j in range(size):
        velocity = [v[i, j, part] for i in range(3)]
        fields = velocity + [a * velocity[0] for a in velocity]
        for end in range(2):
            weight = wtab[end * (size + 4) + j + 2]
            for f in range(6):
                term = weight * fields[f]
                ends[end][f] = term if ends[end][f] is None else ends[end][f] + term
    for end in range(2):
        for f in range(6):
            xe[end, f, part] = ends[end][f]


def x_halo(t, size, xh, wtab, xe):
    part = pl.ds(pl.multiple_of(t * 8, 8), 8)
    ends = [[xe[end, f, part] for f in range(6)] for end in range(2)]
    for side in range(2):
        for layer in range(2):
            j = layer - 2 if side == 0 else size + layer
            velocity = [xh[side, i, layer, part] for i in range(3)]
            fields = velocity + [a * velocity[0] for a in velocity]
            for end in range(2):
                weight = wtab[end * (size + 4) + j + 2]
                for f in range(6):
                    ends[end][f] = ends[end][f] + weight * fields[f]
    for end in range(2):
        for f in range(6):
            xe[end, f, part] = ends[end][f]


def along_y(p, v, parts, ytab, gyz, cyz):
    cz = v.shape[3]
    planes = (2 * p, 2 * p + 1)

    def apply(pieces):
        high = jnp.concatenate([a[0] for a in pieces], axis=1)
        low = jnp.concatenate([a[1] for a in pieces], axis=1)
        return dot(ytab[...], jnp.concatenate([high, low, high], axis=0))

    def held(field):
        got = [parts[field, x] for x in planes]
        return [(g[:, :cz], g[:, cz:]) for g in got]

    for i in range(3):
        got = apply(held(i))
        for k, x in enumerate(planes):
            gyz[0, i, x] = got[:, k * cz : (k + 1) * cz]
        got = apply(held(4) if i == 2 else [split(v[i, x] * v[1, x]) for x in planes])
        for k, x in enumerate(planes):
            cyz[i, x] = got[:, k * cz : (k + 1) * cz]


def along_z(x, parts, ztab, spread, z_rows, gyz, cyz):
    cz = gyz.shape[4]
    high, low = split(z_rows[x])
    extra = dot(jnp.concatenate([high, low, high], axis=0), spread[...], ((0,), (0,)))
    for field in range(6):
        got = dot(parts[field, x], ztab[...])
        got = got[:, :cz] + got[:, cz:] + extra[:, field * cz : (field + 1) * cz]
        if field < 3:
            gyz[1, field, x] = got
        else:
            cyz[field - 3, x] = cyz[field - 3, x] + got


def exchange_kernel(
    v_hbm, xi_hbm, yi_hbm, zi_hbm, mx_hbm, my_hbm, mz_hbm,
    v, xh, xp, xe, tab, gyz, cyz,
    xi, yi, zi, mx, my, mz, xcs, xc, wtab, sel, parts, zs1, zs2, zh, zp, z_rows, ytab, ztab, spread,
    load_sem, x1s, x1r, x2s, x2r, z1s, z1r, z2s, z2r, xcsem, xcrecv,
):
    gx, gy, gz = lax.axis_index("gx"), lax.axis_index("gy"), lax.axis_index("gz")
    nx, ny, nz = lax.axis_size("gx"), lax.axis_size("gy"), lax.axis_size("gz")
    me = gx * ny + gy
    count = nx * ny
    xl, xr = lax.rem(me + count - 1, count), lax.rem(me + 1, count)
    left = {"gx": xl // ny, "gy": lax.rem(xl, ny)}
    right = {"gx": xr // ny, "gy": lax.rem(xr, ny)}
    below = {"gz": lax.rem(gz + nz - 1, nz)}
    above = {"gz": lax.rem(gz + 1, nz)}
    barrier = pltpu.get_barrier_semaphore()
    for device in (left, right, below, above):
        pl.semaphore_signal(barrier, inc=1, device_id=device, device_id_type=MESH)

    loads = [
        pltpu.make_async_copy(src, dst, load_sem.at[k])
        for k, (src, dst) in enumerate(
            ((zi_hbm, zi), (xi_hbm, xi), (v_hbm, v), (yi_hbm, yi), (mx_hbm, mx), (my_hbm, my), (mz_hbm, mz)))
    ]
    for load in loads:
        load.start()
    cx, rows, cz = v.shape[1:]

    def send(src, dst, s, r, device):
        return pltpu.make_async_remote_copy(
            src_ref=src, dst_ref=dst, send_sem=s, recv_sem=r, device_id=device, device_id_type=MESH)

    step = rows // CHUNKS
    pl.semaphore_wait(barrier, 4)
    faces = []
    for c in range(CHUNKS):
        part = pl.ds(c * step, step)
        pair = (
            send(v_hbm.at[:, pl.ds(cx - 2, 2), part], xh.at[0, :, :, part], x1s.at[0, c], x1r.at[0, c], right),
            send(v_hbm.at[:, pl.ds(0, 2), part], xh.at[1, :, :, part], x1s.at[1, c], x1r.at[1, c], left),
        )
        for copy in pair:
            copy.start()
        faces.append(pair)

    loads[0].wait()
    z_inverse = zi[...]
    z_select(z_inverse, sel)
    corner = (z_inverse[0:1, 0:1], z_inverse[cz - 1 : cz, cz - 1 : cz])
    loads[1].wait()
    x_inverse = xi[...]
    xcs[0] = full(x_inverse[0:1, 0:1])
    xcs[1] = full(x_inverse[cx - 1 : cx, cx - 1 : cx])
    corners = (
        send(xcs.at[1], xc.at[0], xcsem.at[0], xcrecv.at[0], right),
        send(xcs.at[0], xc.at[1], xcsem.at[1], xcrecv.at[1], left),
    )
    for copy in corners:
        copy.start()
    loads[2].wait()
    pl.loop(0, cx)(lambda x: z_local(x, v, sel, corner, parts, zs1, zs2))
    z_faces = (
        send(zs1.at[1], zh.at[0], z1s.at[0], z1r.at[0], above),
        send(zs1.at[0], zh.at[1], z1s.at[1], z1r.at[1], below),
    )
    for copy in z_faces:
        copy.start()

    x_end_weights(x_inverse, wtab)
    pl.loop(0, rows // 8)(lambda t: x_local(t, v, wtab, xe))
    for load in loads[3:]:
        load.wait()
    ytab[...] = y_table(yi[...], my[...])

    for copy in z_faces:
        copy.wait()
    high, low = split(z_end_weights(z_inverse))
    wz = jnp.concatenate([high, high, low], axis=1)
    pl.loop(0, cx)(lambda x: z_halo(x, zh, wz, z_rows, zs2))
    z_ends = (
        send(zs2.at[1], zp.at[0], z2s.at[0], z2r.at[0], above),
        send(zs2.at[0], zp.at[1], z2s.at[1], z2r.at[1], below),
    )
    for copy in z_ends:
        copy.start()

    x_ends = []
    done = 0
    for c in range(CHUNKS):
        for copy in faces[c]:
            copy.wait()
        pl.loop(c * (step // 8), (c + 1) * (step // 8))(lambda t: x_halo(t, cx, xh, wtab, xe))
        part = pl.ds(c * step, step)
        pair = (
            send(xe.at[1, :, part], xp.at[0, :, part], x2s.at[0, c], x2r.at[0, c], right),
            send(xe.at[0, :, part], xp.at[1, :, part], x2s.at[1, c], x2r.at[1, c], left),
        )
        for copy in pair:
            copy.start()
        x_ends.append(pair)
        if c < CHUNKS - 1:
            pl.loop(done, done + BETWEEN)(lambda p: along_y(p, v, parts, ytab, gyz, cyz))
            done += BETWEEN

    pl.loop(done, cx // 2)(lambda p: along_y(p, v, parts, ytab, gyz, cyz))
    for copy in z_ends:
        copy.wait()
    for side in range(2):
        z_rows[:, 32 + 8 * side : 40 + 8 * side] = zp[side]
    z_tables(z_inverse, mz[...], zh[0, 0, 6:7, 0:1], zh[1, 0, 6:7, 0:1], ztab, spread)
    pl.loop(0, cx)(lambda x: along_z(x, parts, ztab, spread, z_rows, gyz, cyz))
    for copy in corners:
        copy.wait()
    x_tables(x_inverse, mx[...], xc, tab)
    for pair in x_ends:
        for copy in pair:
            copy.wait()


def exchange(velocity, x_inverse, y_inverse, z_inverse, metric_x, metric_y, metric_z):
    _, cx, rows, cz = velocity.shape
    dma = pltpu.SemaphoreType.DMA

    def vmem(*shape):
        return pltpu.VMEM(shape, F32)

    def half(*shape):
        return pltpu.VMEM(shape, BF16)

    outs = (
        (3, cx, rows, cz),
        (2, 3, 2, rows, cz),
        (2, 6, rows, cz),
        (2, 6, rows, cz),
        (3 * cx + 4, 8, 128),
        (2, 3, cx, rows, cz),
        (3, cx, rows, cz),
    )
    return pl.pallas_call(
        exchange_kernel,
        out_shape=tuple(jax.ShapeDtypeStruct(shape, F32) for shape in outs),
        in_specs=[pl.BlockSpec(memory_space=pltpu.HBM)] * 7,
        out_specs=(pl.BlockSpec(memory_space=pltpu.VMEM),) * len(outs),
        scratch_shapes=[
            vmem(cx, cx), vmem(rows, rows), vmem(cz, cz), vmem(1, cx), vmem(1, rows), vmem(1, cz),
            vmem(2, 8, 128), vmem(2, 8, 128), vmem(2 * (cx + 4), 8, 128),
            half(6, 64, 2 * cz), half(6, cx, rows, 2 * cz),
            vmem(2, cx, 8, rows), vmem(2, cx, 8, rows), vmem(2, cx, 8, rows), vmem(2, cx, 8, rows),
            vmem(cx, 64, rows),
            half(rows, 3 * rows), half(2 * cz, 2 * cz), half(192, 6 * cz),
            dma((7,)),
            dma((2, CHUNKS)), dma((2, CHUNKS)), dma((2, CHUNKS)), dma((2, CHUNKS)),
            dma((2,)), dma((2,)), dma((2,)), dma((2,)), dma((2,)), dma((2,)),
        ],
        compiler_params=pltpu.CompilerParams(
            collective_id=0, has_side_effects=True, vmem_limit_bytes=22 * MIB),
        name="exchange",
    )(*[
        pltpu.with_memory_space_constraint(a, pltpu.HBM)
        for a in (velocity, x_inverse, y_inverse, z_inverse, metric_x.reshape(1, cx),
                  metric_y.reshape(1, rows), metric_z.reshape(1, cz))
    ])


def x_sweep(part, v, xh, xp, xe, tab, gx, conv, cyz):
    cx = v.shape[1]

    def cell(j):
        if j < 0:
            velocity = [xh[0, i, j + 2, part] for i in range(3)]
        elif j >= cx:
            velocity = [xh[1, i, j - cx, part] for i in range(3)]
        else:
            velocity = [v[i, j, part] for i in range(3)]
        return velocity + [a * velocity[0] for a in velocity]

    window = [cell(j) for j in range(-2, 2)]
    state = None
    for j in range(cx):
        window.append(cell(j + 2))
        fresh = []
        for f in range(6):
            d = (window[3][f] - window[1][f]) + (FAR / NEAR) * (window[4][f] - window[0][f])
            for side, line in ((0, 0), (1, cx - 1)):
                if j == line:
                    k = 3 * cx + 2 * side
                    d = d - tab[k] * xp[side, f, part] + tab[k + 1] * xe[side, f, part]
            value = tab[j] * d
            if state is not None:
                value = value + tab[cx + j] * state[f]
            fresh.append(value)
            if j < cx - 1:
                if f < 3:
                    gx[f, j, part] = value
                else:
                    conv[f - 3, j, part] = value
        state = fresh
        window.pop(0)
    for j in range(cx - 1, -1, -1):
        if j < cx - 1:
            up = tab[2 * cx + j]
            state = [(gx[f, j, part] if f < 3 else conv[f - 3, j, part]) + up * state[f] for f in range(6)]
        for i in range(3):
            gx[i, j, part] = state[i]
            conv[i, j, part] = state[3 + i] + cyz[i, j, part]


def x_kernel(v, xh, xp, xe, tab, gyz, cyz, grad, conv, gx_out, conv_out, yz_sem, x_sem, c_sem):
    rows = v.shape[2]
    copies = [pltpu.make_async_copy(gyz.at[k], grad.at[:, 1 + k], yz_sem.at[k]) for k in range(2)]
    for copy in copies:
        copy.start()
    step = rows // OUT_CHUNKS
    for c in range(OUT_CHUNKS):
        @pl.loop(c * (step // 8), (c + 1) * (step // 8))
        def _(t):
            x_sweep(pl.ds(pl.multiple_of(t * 8, 8), 8), v, xh, xp, xe, tab, gx_out, conv_out, cyz)

        part = pl.ds(c * step, step)
        pair = (
            pltpu.make_async_copy(gx_out.at[:, :, part], grad.at[:, 0, :, part], x_sem.at[c]),
            pltpu.make_async_copy(conv_out.at[:, :, part], conv.at[:, :, part], c_sem.at[c]),
        )
        for copy in pair:
            copy.start()
        copies += pair
    for copy in copies:
        copy.wait()


def x_solve(v, xh, xp, xe, tab, gyz, cyz):
    _, cx, rows, cz = v.shape
    dma = pltpu.SemaphoreType.DMA
    return pl.pallas_call(
        x_kernel,
        out_shape=(
            jax.ShapeDtypeStruct((3, 3, cx, rows, cz), F32),
            jax.ShapeDtypeStruct((3, cx, rows, cz), F32),
        ),
        in_specs=[pl.BlockSpec(memory_space=pltpu.VMEM)] * 7,
        out_specs=(pl.BlockSpec(memory_space=pltpu.HBM),) * 2,
        scratch_shapes=[
            pltpu.VMEM((3, cx, rows, cz), F32),
            pltpu.VMEM((3, cx, rows, cz), F32),
            dma((2,)), dma((OUT_CHUNKS,)), dma((OUT_CHUNKS,)),
        ],
        compiler_params=pltpu.CompilerParams(vmem_limit_bytes=14 * MIB),
        name="x_solve",
    )(v, xh, xp, xe, tab, gyz, cyz)


def on_device(velocity, metric_x, metric_y, metric_z, x_inverse, y_inverse, z_inverse):
    return tuple(x_solve(*exchange(
        velocity, x_inverse, y_inverse, z_inverse, metric_x, metric_y, metric_z)))


def solution(mesh):
    return jax.shard_map(
        on_device,
        mesh=mesh,
        in_specs=(
            P(None, ("gx", "gy"), None, "gz"),
            P(("gx", "gy")),
            P(),
            P("gz"),
            P(("gx", "gy"), None),
            P(),
            P("gz", None),
        ),
        out_specs=(P(None, None, ("gx", "gy"), None, "gz"), P(None, ("gx", "gy"), None, "gz")),
        check_vma=False,
    )
```

time: 357 us -> 41 us (0.11); the launches traced: 353 us -> 40.9 us
  other arithmetic: 149 us -> 0 us
  local copies, waits for them, and re-layouts: 114 us -> 0 us
  matrix products: 69 us -> 0 us
  Pallas kernels: 0 us -> 40.3 us
  starting transfers between devices: 17 us -> 0 us
    dot_general x3 -> x0, matrix products: 69 us -> none  [block_solve(): return jnp.einsum(form, inverse, source, precision=lax.Precision.HIGHEST)]
    mul x10 -> x0, other arithmetic: 59.4 us -> none  [the longest x3 18 us: direction_fields(): velocity * velocity[direction:direction + 1]]
    slice x10 -> x0, local copies, waits for them, and re-layouts: 42.6 us -> none  [the longest x4 28.3 us: pick(): return lax.slice_in_dim(values, position, position + 1, axis=axis_of)]
    pallas_call x0 -> x2, Pallas kernels: none -> 40.3 us  [the longest x1 33.7 us: exchange(): pl.pallas_call(exchange_kernel, out_shape=tuple((jax.ShapeDtypeStruct(sha...]
    unnamed x47 -> x0, local copies, waits for them, and re-layouts: 38.4 us -> none
    add x2 -> x0, other arithmetic: 31 us -> none  [the longest x1 17.4 us: on_device(): convection = result_x[3:] + result_y[3:] + result_z[3:]]
    div x5 -> x0, other arithmetic: 25.3 us -> none  [the longest x3 15.2 us: combine_ends(): (left_value - COUPLING * left_tail * own_head) / (1.0 - COUPLING * COUPLI...]
    mul x5 -> x0, local copies, waits for them, and re-layouts: 21 us -> none  [the longest x1 8.92 us: combine_ends(): COUPLING * column_first * left_final]
  transfers between devices with their start and end apart: 8 -> 0, of which waited for: 0 -> 0; matrix products, arithmetic and copies ran while one was open for 50% -> 0% of each run, Pallas kernels for 0% -> 0%
where the time goes in v2:
time: 41 us; the launch traced here: 40.9 us
  Pallas kernels  40.3 us (98%)
  between operations  0.64 us (2%)
    pallas_call x1, Pallas kernels, exchange(): pl.pallas_call(exchange_kernel, out_shape=tuple((jax.ShapeDtypeStruct(sha...  33.7 us
    pallas_call x1, Pallas kernels, x_solve(): pl.pallas_call(x_kernel, out_shape=(jax.ShapeDtypeStruct((3, 3, cx, rows,...  6.58 us

profile of v2, /device:TPU:0, one launch (start us, length us, event | category | flops | bytes accessed | tf_op | source)
XLA Modules:
  0.0 40.9 jit_solution(15586960217171155031)
XLA Ops:
  0.6 33.7 %exchange.1 = (f32[3,16,192,128]{3,2,1,0:T(8,128)S(1)}, f32[2,3,2,192,128]{4,3,2,1,0:T(8,128)S(1)}, f32[2,6,192,128]{3,2,1,0:T(8,128)S(1)}, f32[2,6,192,128]{3,2...) custom-call(f32[3,16,192,128]{3,2,1,0:T(8,128)} %v_hbm.1, ...), custom_call_target="tpu_custom_call" | custom-call | tf_op jit(solution)/shard_map/exchange/pallas_call | solution.py:407
  34.3 6.6 %x_solve.1 = (f32[3,3,16,192,128]{4,3,2,1,0:T(8,128)}, f32[3,16,192,128]{3,2,1,0:T(8,128)}) custom-call(f32[3,16,192,128]{3,2,1,0:T(8,128)S(1)} %get-tuple-element.9.v, f32[2,3,2,192,128]{4,3,2,1,0:T(8,128)S(1)} %get-tuple-element.10.xh, f32[2,6,192,128]{3,2,1,0:T(8,128)S(1)} %get-tuple-element.11.xp, f32[2,6,192,128]{3,2,1,0:T(8,128)S(1)} %get-tuple-element.12.xe, ...), custom_call_target="tpu_custom_call" | custom-call | tf_op jit(solution)/shard_map/x_solve/pallas_call | solution.py:502

commit v3 on v2

v3 whole, which is shorter than its diff:
```python
import jax
import jax.numpy as jnp
from jax import lax
from jax.experimental import pallas as pl
from jax.experimental.pallas import tpu as pltpu
from jax.sharding import PartitionSpec as P

COUPLING = 1.0 / 3.0
NEAR = 7.0 / 9.0
FAR = 1.0 / 36.0
F32 = jnp.float32
BF16 = jnp.bfloat16
MESH = pl.DeviceIdType.MESH
HIGH = lax.Precision.HIGHEST
CHUNKS = 2
OUT_CHUNKS = 6
MIB = 1 << 20


def split(values):
    high = values.astype(BF16)
    return high, (values - high.astype(F32)).astype(BF16)


def iota(shape, dim):
    return lax.broadcasted_iota(jnp.int32, shape, dim)


def band(size):
    step = iota((size, size), 1) - iota((size, size), 0)
    near = jnp.where(step == 1, NEAR, jnp.where(step == -1, -NEAR, 0.0))
    far = jnp.where(step == 2, FAR, jnp.where(step == -2, -FAR, 0.0))
    return (near + far).astype(F32)


def dot(a, b, dims=((1,), (0,)), precision=None):
    return lax.dot_general(a, b, (dims, ((), ())), precision=precision, preferred_element_type=F32)


def z_tables(z_inverse, metric, spread):
    size = z_inverse.shape[0]
    columns = z_inverse.T
    lines = [columns[k : k + 1] * metric for k in (0, 1, size - 2, size - 1)]
    row = iota((32, size), 0)
    zero = jnp.zeros((64, size), BF16)
    for field in range(6):
        table = jnp.zeros((32, size), F32)
        for k, line in enumerate(lines):
            table = jnp.where(row == 8 * k + field, line, table)
        high, low = split(table)
        spread[:, field * size : (field + 1) * size] = jnp.concatenate(
            [high, high, zero, low, low, zero], axis=0)


def z_weights(z_inverse, metric, weights):
    high, low = split(dot(z_inverse, band(z_inverse.shape[0]), precision=HIGH).T * metric)
    both = jnp.concatenate([high, low], axis=1)
    weights[...] = jnp.concatenate([both, both], axis=0)


def y_table(y_inverse, metric):
    size = y_inverse.shape[0]
    own = iota((size, size), 0) == iota((size, size), 1)
    column = jnp.sum(jnp.where(own, metric, 0.0), axis=1, keepdims=True)
    high, low = split(y_inverse)
    near, rest = split(band(size))
    product = dot(jnp.concatenate([high, low, high], axis=1), jnp.concatenate([near, near, rest], axis=0))
    high, low = split(product * column)
    return jnp.concatenate([high, high, low], axis=1)


def x_end_weights(inverse, store):
    size = inverse.shape[0]
    rows = size + 8
    step = iota((rows, size), 0) - iota((rows, size), 1) - 2
    near = jnp.where(step == 1, NEAR, jnp.where(step == -1, -NEAR, 0.0))
    far = jnp.where(step == 2, FAR, jnp.where(step == -2, -FAR, 0.0))
    taps = (near + far).astype(F32)
    for end, line in ((0, 0), (1, size - 1)):
        column = jnp.sum(taps * inverse[line : line + 1], axis=1, keepdims=True)
        store[end * rows : (end + 1) * rows] = jnp.broadcast_to(column, (rows, 128))


def x_tables(inverse, metric, corners, tab):
    size = inverse.shape[0]
    row, col = iota((size, size), 0), iota((size, size), 1)

    def pick(values, shift):
        return jnp.sum(jnp.where(col == row + shift, values, 0.0), axis=1, keepdims=True)

    def shifted(values, by):
        pad = jnp.zeros((1, values.shape[1]), F32)
        if by > 0:
            return jnp.concatenate([values[1:], pad], axis=0)
        return jnp.concatenate([pad, values[:-1]], axis=0)

    line = iota((size, 1), 0)
    below = shifted(inverse, 1)
    scale = pick(metric, 0)
    pivot = jnp.where(line < size - 1, pick(below, 1), 1.0)
    up = pick(inverse, 1) / pivot
    own = pick(inverse, 0) - up * pick(below, 0)
    before = jnp.where(line > 0, shifted(own, -1), 1.0)
    down = (pick(inverse, -1) - up * pick(below, -1)) / before
    above_scale = jnp.where(line < size - 1, pick(metric, 1), 1.0)
    below_scale = jnp.where(line > 0, pick(metric, -1), 1.0)
    for k, value in enumerate((NEAR * scale * own, down * scale / below_scale, up * scale / above_scale)):
        tab[k * size : (k + 1) * size] = jnp.broadcast_to(value, (size, 128))
    for side, end in ((0, 0), (1, size - 1)):
        own_end = inverse[end : end + 1, end : end + 1]
        other = corners[side]
        gain = (COUPLING / NEAR) / (1.0 - COUPLING * COUPLING * other * own_end)
        tab[3 * size + 16 * side : 3 * size + 16 * side + 8] = gain
        tab[3 * size + 16 * side + 8 : 3 * size + 16 * side + 16] = COUPLING * other * gain


def tile_of(table, row):
    return jnp.broadcast_to(table[row : row + 1], (8, 128))


def z_faces_of(v, corner, zs1):
    size, rows = v.shape[1:3]
    lane = iota((1, 128), 1)
    for k in range(2 * rows // 128):
        total = None
        for p in range(size // 2):
            for i in range(3):
                lines = v[i, 2 * p : 2 * p + 2].reshape(2 * rows, 128)[128 * k : 128 * k + 128]
                first = 16 * p + 4 * i
                moved = pltpu.roll(lines, first + 2, 1)
                total = moved if total is None else jnp.where((lane >= first) & (lane < first + 4), moved, total)
        got = total.T
        for p in range(size // 2):
            for side, layers in ((0, (2, 3)), (1, (0, 1))):
                lines = [got[16 * p + 4 * i + n : 16 * p + 4 * i + n + 1] for n in layers for i in range(3)]
                zs1[side, p, :, 128 * k : 128 * k + 128] = jnp.concatenate(
                    lines + [jnp.broadcast_to(corner[side], (1, 128)), jnp.zeros((1, 128), F32)], axis=0)


def z_ends_of(gather, inverse_metric, zs2):
    for k in range(gather.shape[0] // 128):
        got = gather[128 * k : 128 * k + 128].T
        for p in range(zs2.shape[1]):
            for side in range(2):
                lines = [got[16 * p + 2 * f + 1 - side : 16 * p + 2 * f + 2 - side] for f in range(6)]
                zs2[side, p, :, 128 * k : 128 * k + 128] = inverse_metric[side] * jnp.concatenate(
                    lines + [jnp.zeros((2, 128), F32)], axis=0)


def z_local(p, v, parts, ztab, gyz, cyz, gather):
    rows, cz = v.shape[2:]
    lane = iota((1, cz), 1)
    for k in range(2):
        x = 2 * p + k
        velocity = [v[i, x] for i in range(3)]
        for field in range(6):
            value = velocity[field] if field < 3 else velocity[field - 3] * velocity[2]
            parts[field, x] = jnp.concatenate(split(value), axis=1)
        got = dot(parts[:, x].reshape(6 * rows, 2 * cz), ztab[...])
        got = got[:, :cz] + got[:, cz:]
        ends = gather[k * rows : (k + 1) * rows]
        for f in range(6):
            values = got[f * rows : (f + 1) * rows]
            if f < 3:
                gyz[1, f, x] = values
            else:
                cyz[f - 3, x] = values
            first = 16 * p + 2 * f
            ends = jnp.where((lane >= first) & (lane < first + 2), pltpu.roll(values, first + 1, 1), ends)
        gather[k * rows : (k + 1) * rows] = ends


def beside(halo, near, far):
    def six(first):
        lines = halo[first : first + 3]
        pad = jnp.zeros((2, lines.shape[1]), F32)
        return jnp.concatenate([lines, lines * lines[2:3], pad], axis=0)

    return six(near), six(far)


def z_halo(zh, z_inverse, zs2):
    size = z_inverse.shape[0]
    weights = []
    for line in (0, size - 1):
        a, b, c, d = (z_inverse[line : line + 1, k : k + 1] for k in (0, 1, size - 2, size - 1))
        weights.append((-NEAR * a - FAR * b, -FAR * a, NEAR * d + FAR * c, FAR * d))
    for p in range(zh.shape[1]):
        layers = beside(zh[0, p], 3, 0) + beside(zh[1, p], 0, 3)
        for side in range(2):
            total = zs2[side, p]
            for weight, layer in zip(weights[side], layers):
                total = total + weight * layer
            zs2[side, p] = total


def z_correct(q, spread, z_inverse, zh, zp, zs2, gyz, cyz):
    rows, cz = gyz.shape[3:]
    square = COUPLING * COUPLING
    own = (z_inverse[0:1, 0:1], z_inverse[cz - 1 : cz, cz - 1 : cz])
    lines = []
    for k in range(2):
        p = 2 * q + k
        terms = []
        for side, sign in ((0, -1.0), (1, 1.0)):
            halo = zh[side, p]
            near, far = beside(halo, 3 - 3 * side, 3 * side)
            other = halo[6:7, 0:1]
            gain = COUPLING / (1.0 - square * other * own[side])
            first = (sign * NEAR) * near + (sign * FAR) * far - gain * zp[side, p]
            first = first + (COUPLING * other * gain) * zs2[side, p]
            second = (sign * FAR) * near
            terms += [first, second] if side == 0 else [second, first]
        high, low = split(jnp.concatenate(terms, axis=0))
        lines += [high.astype(F32), low.astype(F32)]
    turned = jnp.concatenate(lines, axis=0).T
    turned = jnp.concatenate([turned, pltpu.roll(turned, 64, 1)], axis=0).astype(BF16)
    more = dot(jnp.concatenate([turned, turned], axis=1), spread[...])
    planes = pl.ds(4 * q, 4)
    for i in range(3):
        gyz[1, i, planes] = gyz[1, i, planes] + more[:, i * cz : (i + 1) * cz].reshape(4, rows, cz)
        cyz[i, planes] = cyz[i, planes] + more[:, (3 + i) * cz : (4 + i) * cz].reshape(4, rows, cz)


def x_local(t, v, wtab, xe):
    part = pl.ds(pl.multiple_of(t * 8, 8), 8)
    size = v.shape[1]
    ends = [[None] * 6, [None] * 6]
    for j in range(size):
        velocity = [v[i, j, part] for i in range(3)]
        fields = velocity + [a * velocity[0] for a in velocity]
        for end in range(2):
            weight = tile_of(wtab, end * (size + 8) + j + 2)
            for f in range(6):
                term = weight * fields[f]
                ends[end][f] = term if ends[end][f] is None else ends[end][f] + term
    for end in range(2):
        for f in range(6):
            xe[end, f, part] = ends[end][f]


def x_halo(t, size, xh, wtab, xe):
    part = pl.ds(pl.multiple_of(t * 8, 8), 8)
    ends = [[xe[end, f, part] for f in range(6)] for end in range(2)]
    for side in range(2):
        for layer in range(2):
            j = layer - 2 if side == 0 else size + layer
            velocity = [xh[side, i, layer, part] for i in range(3)]
            fields = velocity + [a * velocity[0] for a in velocity]
            for end in range(2):
                weight = tile_of(wtab, end * (size + 8) + j + 2)
                for f in range(6):
                    ends[end][f] = ends[end][f] + weight * fields[f]
    for end in range(2):
        for f in range(6):
            xe[end, f, part] = ends[end][f]


def along_y(p, v, parts, ytab, gyz, cyz):
    cz = v.shape[3]
    planes = (2 * p, 2 * p + 1)

    def apply(pieces):
        high = jnp.concatenate([a[0] for a in pieces], axis=1)
        low = jnp.concatenate([a[1] for a in pieces], axis=1)
        return dot(ytab[...], jnp.concatenate([high, low, high], axis=0))

    def held(field):
        got = [parts[field, x] for x in planes]
        return [(g[:, :cz], g[:, cz:]) for g in got]

    for i in range(3):
        got = apply(held(i))
        for k, x in enumerate(planes):
            gyz[0, i, x] = got[:, k * cz : (k + 1) * cz]
        got = apply(held(4) if i == 2 else [split(v[i, x] * v[1, x]) for x in planes])
        for k, x in enumerate(planes):
            cyz[i, x] = cyz[i, x] + got[:, k * cz : (k + 1) * cz]


def exchange_kernel(
    v_hbm, xi_hbm, yi_hbm, zi_hbm, mx_hbm, my_hbm, mz_hbm,
    v, xh, xp, xe, tab, gyz, cyz,
    xi, yi, zi, mx, my, mz, xcs, xc, wtab, parts, zs1, zs2, zh, zp, gather, ytab, ztab, spread,
    load_sem, x1s, x1r, x2s, x2r, z1s, z1r, z2s, z2r, xcsem, xcrecv,
):
    gx, gy, gz = lax.axis_index("gx"), lax.axis_index("gy"), lax.axis_index("gz")
    nx, ny, nz = lax.axis_size("gx"), lax.axis_size("gy"), lax.axis_size("gz")
    me = gx * ny + gy
    count = nx * ny
    xl, xr = lax.rem(me + count - 1, count), lax.rem(me + 1, count)
    left = {"gx": xl // ny, "gy": lax.rem(xl, ny)}
    right = {"gx": xr // ny, "gy": lax.rem(xr, ny)}
    below = {"gz": lax.rem(gz + nz - 1, nz)}
    above = {"gz": lax.rem(gz + 1, nz)}
    barrier = pltpu.get_barrier_semaphore()
    for device in (left, right, below, above):
        pl.semaphore_signal(barrier, inc=1, device_id=device, device_id_type=MESH)

    loads = [
        pltpu.make_async_copy(src, dst, load_sem.at[k])
        for k, (src, dst) in enumerate(
            ((zi_hbm, zi), (xi_hbm, xi), (v_hbm, v), (yi_hbm, yi), (mx_hbm, mx), (my_hbm, my), (mz_hbm, mz)))
    ]
    for load in loads:
        load.start()
    cx, rows, cz = v.shape[1:]

    def send(src, dst, s, r, device):
        return pltpu.make_async_remote_copy(
            src_ref=src, dst_ref=dst, send_sem=s, recv_sem=r, device_id=device, device_id_type=MESH)

    step = rows // CHUNKS
    pl.semaphore_wait(barrier, 4)
    faces = []
    for c in range(CHUNKS):
        part = pl.ds(c * step, step)
        pair = (
            send(v_hbm.at[:, pl.ds(cx - 2, 2), part], xh.at[0, :, :, part], x1s.at[0, c], x1r.at[0, c], right),
            send(v_hbm.at[:, pl.ds(0, 2), part], xh.at[1, :, :, part], x1s.at[1, c], x1r.at[1, c], left),
        )
        for copy in pair:
            copy.start()
        faces.append(pair)

    loads[0].wait()
    loads[6].wait()
    z_inverse = zi[...]
    corner = (z_inverse[0:1, 0:1], z_inverse[cz - 1 : cz, cz - 1 : cz])
    z_weights(z_inverse, mz[...], ztab)
    loads[1].wait()
    x_inverse = xi[...]
    xcs[0] = jnp.broadcast_to(x_inverse[0:1, 0:1], (8, 128))
    xcs[1] = jnp.broadcast_to(x_inverse[cx - 1 : cx, cx - 1 : cx], (8, 128))
    corners = (
        send(xcs.at[1], xc.at[0], xcsem.at[0], xcrecv.at[0], right),
        send(xcs.at[0], xc.at[1], xcsem.at[1], xcrecv.at[1], left),
    )
    for copy in corners:
        copy.start()
    loads[2].wait()
    z_faces_of(v, corner, zs1)
    z_faces = (
        send(zs1.at[1], zh.at[0], z1s.at[0], z1r.at[0], above),
        send(zs1.at[0], zh.at[1], z1s.at[1], z1r.at[1], below),
    )
    for copy in z_faces:
        copy.start()

    x_end_weights(x_inverse, wtab)
    pl.loop(0, rows // 8)(lambda t: x_local(t, v, wtab, xe))
    inverse_metric = (1.0 / mz[:, 0:1], 1.0 / mz[:, cz - 1 : cz])

    def z_pass(first, last):
        pl.loop(first, last)(lambda p: z_local(p, v, parts, ztab, gyz, cyz, gather))

    x_ends = []

    def x_pass(c):
        for copy in faces[c]:
            copy.wait()
        pl.loop(c * (step // 8), (c + 1) * (step // 8))(lambda t: x_halo(t, cx, xh, wtab, xe))
        part = pl.ds(c * step, step)
        pair = (
            send(xe.at[1, :, part], xp.at[0, :, part], x2s.at[0, c], x2r.at[0, c], right),
            send(xe.at[0, :, part], xp.at[1, :, part], x2s.at[1, c], x2r.at[1, c], left),
        )
        for copy in pair:
            copy.start()
        x_ends.append(pair)

    z_tables(z_inverse, mz[...], spread)
    gather[...] = jnp.zeros(gather.shape, F32)
    z_pass(0, cx // 4)
    x_pass(0)
    z_pass(cx // 4, cx // 2)
    for copy in z_faces:
        copy.wait()
    z_ends_of(gather, inverse_metric, zs2)
    z_halo(zh, z_inverse, zs2)
    z_ends = (
        send(zs2.at[1], zp.at[0], z2s.at[0], z2r.at[0], above),
        send(zs2.at[0], zp.at[1], z2s.at[1], z2r.at[1], below),
    )
    for copy in z_ends:
        copy.start()
    for c in range(1, CHUNKS):
        x_pass(c)

    for load in loads[3:6]:
        load.wait()
    ytab[...] = y_table(yi[...], my[...])
    pl.loop(0, cx // 2)(lambda p: along_y(p, v, parts, ytab, gyz, cyz))
    for copy in z_ends:
        copy.wait()
    pl.loop(0, cx // 4)(lambda q: z_correct(q, spread, z_inverse, zh, zp, zs2, gyz, cyz))
    for copy in corners:
        copy.wait()
    x_tables(x_inverse, mx[...], xc, tab)
    for pair in x_ends:
        for copy in pair:
            copy.wait()


def exchange(velocity, x_inverse, y_inverse, z_inverse, metric_x, metric_y, metric_z):
    _, cx, rows, cz = velocity.shape
    dma = pltpu.SemaphoreType.DMA

    def vmem(*shape):
        return pltpu.VMEM(shape, F32)

    def half(*shape):
        return pltpu.VMEM(shape, BF16)

    outs = (
        (3, cx, rows, cz),
        (2, 3, 2, rows, cz),
        (2, 6, rows, cz),
        (2, 6, rows, cz),
        (3 * cx + 32, 128),
        (2, 3, cx, rows, cz),
        (3, cx, rows, cz),
    )
    return pl.pallas_call(
        exchange_kernel,
        out_shape=tuple(jax.ShapeDtypeStruct(shape, F32) for shape in outs),
        in_specs=[pl.BlockSpec(memory_space=pltpu.HBM)] * 7,
        out_specs=(pl.BlockSpec(memory_space=pltpu.VMEM),) * len(outs),
        scratch_shapes=[
            vmem(cx, cx), vmem(rows, rows), vmem(cz, cz), vmem(1, cx), vmem(1, rows), vmem(1, cz),
            vmem(2, 8, 128), vmem(2, 8, 128), vmem(2 * (cx + 8), 128),
            half(6, cx, rows, 2 * cz),
            *[vmem(2, cx // 2, 8, 2 * rows)] * 4, vmem(2 * rows, cz),
            half(rows, 3 * rows), half(2 * cz, 2 * cz), half(256, 6 * cz),
            dma((7,)),
            dma((2, CHUNKS)), dma((2, CHUNKS)), dma((2, CHUNKS)), dma((2, CHUNKS)),
            dma((2,)), dma((2,)), dma((2,)), dma((2,)), dma((2,)), dma((2,)),
        ],
        compiler_params=pltpu.CompilerParams(
            collective_id=0, has_side_effects=True, vmem_limit_bytes=22 * MIB),
        name="exchange",
    )(*[
        pltpu.with_memory_space_constraint(a, pltpu.HBM)
        for a in (velocity, x_inverse, y_inverse, z_inverse, metric_x.reshape(1, cx),
                  metric_y.reshape(1, rows), metric_z.reshape(1, cz))
    ])


def x_sweep(part, v, xh, xp, xe, tab, gx, conv, cyz):
    cx = v.shape[1]

    def cell(j):
        if j < 0:
            velocity = [xh[0, i, j + 2, part] for i in range(3)]
        elif j >= cx:
            velocity = [xh[1, i, j - cx, part] for i in range(3)]
        else:
            velocity = [v[i, j, part] for i in range(3)]
        return velocity + [a * velocity[0] for a in velocity]

    window = [cell(j) for j in range(-2, 2)]
    state = None
    for j in range(cx):
        window.append(cell(j + 2))
        fresh = []
        for f in range(6):
            d = (window[3][f] - window[1][f]) + (FAR / NEAR) * (window[4][f] - window[0][f])
            for side, line in ((0, 0), (1, cx - 1)):
                if j == line:
                    k = 3 * cx + 16 * side
                    d = d - tab[k : k + 8] * xp[side, f, part] + tab[k + 8 : k + 16] * xe[side, f, part]
            value = tile_of(tab, j) * d
            if state is not None:
                value = value + tile_of(tab, cx + j) * state[f]
            fresh.append(value)
            if j < cx - 1:
                if f < 3:
                    gx[f, j, part] = value
                else:
                    conv[f - 3, j, part] = value
        state = fresh
        window.pop(0)
    for j in range(cx - 1, -1, -1):
        if j < cx - 1:
            up = tile_of(tab, 2 * cx + j)
            state = [(gx[f, j, part] if f < 3 else conv[f - 3, j, part]) + up * state[f] for f in range(6)]
        for i in range(3):
            gx[i, j, part] = state[i]
            conv[i, j, part] = state[3 + i] + cyz[i, j, part]


def x_kernel(v, xh, xp, xe, tab, gyz, cyz, grad, conv, gx_out, conv_out, yz_sem, x_sem, c_sem):
    rows = v.shape[2]
    copies = [pltpu.make_async_copy(gyz.at[k], grad.at[:, 1 + k], yz_sem.at[k]) for k in range(2)]
    for copy in copies:
        copy.start()
    step = rows // OUT_CHUNKS
    for c in range(OUT_CHUNKS):
        @pl.loop(c * (step // 8), (c + 1) * (step // 8))
        def _(t):
            x_sweep(pl.ds(pl.multiple_of(t * 8, 8), 8), v, xh, xp, xe, tab, gx_out, conv_out, cyz)

        part = pl.ds(c * step, step)
        pair = (
            pltpu.make_async_copy(gx_out.at[:, :, part], grad.at[:, 0, :, part], x_sem.at[c]),
            pltpu.make_async_copy(conv_out.at[:, :, part], conv.at[:, :, part], c_sem.at[c]),
        )
        for copy in pair:
            copy.start()
        copies += pair
    for copy in copies:
        copy.wait()


def x_solve(v, xh, xp, xe, tab, gyz, cyz):
    _, cx, rows, cz = v.shape
    dma = pltpu.SemaphoreType.DMA
    return pl.pallas_call(
        x_kernel,
        out_shape=(
            jax.ShapeDtypeStruct((3, 3, cx, rows, cz), F32),
            jax.ShapeDtypeStruct((3, cx, rows, cz), F32),
        ),
        in_specs=[pl.BlockSpec(memory_space=pltpu.VMEM)] * 7,
        out_specs=(pl.BlockSpec(memory_space=pltpu.HBM),) * 2,
        scratch_shapes=[
            pltpu.VMEM((3, cx, rows, cz), F32),
            pltpu.VMEM((3, cx, rows, cz), F32),
            dma((2,)), dma((OUT_CHUNKS,)), dma((OUT_CHUNKS,)),
        ],
        compiler_params=pltpu.CompilerParams(vmem_limit_bytes=14 * MIB),
        name="x_solve",
    )(v, xh, xp, xe, tab, gyz, cyz)


def on_device(velocity, metric_x, metric_y, metric_z, x_inverse, y_inverse, z_inverse):
    return tuple(x_solve(*exchange(
        velocity, x_inverse, y_inverse, z_inverse, metric_x, metric_y, metric_z)))


def solution(mesh):
    return jax.shard_map(
        on_device,
        mesh=mesh,
        in_specs=(
            P(None, ("gx", "gy"), None, "gz"),
            P(("gx", "gy")),
            P(),
            P("gz"),
            P(("gx", "gy"), None),
            P(),
            P("gz", None),
        ),
        out_specs=(P(None, None, ("gx", "gy"), None, "gz"), P(None, ("gx", "gy"), None, "gz")),
        check_vma=False,
    )
```

time: 41 us -> 33.1 us (0.81)
  Pallas kernels: 40.3 us -> 32.3 us
    pallas_call x1, Pallas kernels: 33.7 us -> 25.7 us  [exchange(): pl.pallas_call(exchange_kernel, out_shape=tuple((jax.ShapeDtypeStruct(sha...]
where the time goes in v3:
time: 33.1 us; the launch traced here: 33 us
  Pallas kernels  32.3 us (98%)
  between operations  0.64 us (2%)
    pallas_call x1, Pallas kernels, exchange(): pl.pallas_call(exchange_kernel, out_shape=tuple((jax.ShapeDtypeStruct(sha...  25.7 us
    pallas_call x1, Pallas kernels, x_solve(): pl.pallas_call(x_kernel, out_shape=(jax.ShapeDtypeStruct((3, 3, cx, rows,...  6.58 us

profile of v3, /device:TPU:0, one launch (start us, length us, event | category | flops | bytes accessed | tf_op | source)
XLA Modules:
  0.0 33.0 jit_solution(5884195370585237463)
XLA Ops:
  0.6 25.7 %exchange.1 = (f32[3,16,192,128]{3,2,1,0:T(8,128)S(1)}, f32[2,3,2,192,128]{4,3,2,1,0:T(8,128)S(1)}, f32[2,6,192,128]{3,2,1,0:T(8,128)S(1)}, f32[2,6,192,128]{3,2...) custom-call(f32[3,16,192,128]{3,2,1,0:T(8,128)} %v_hbm.1, ...), custom_call_target="tpu_custom_call" | custom-call | tf_op jit(solution)/shard_map/exchange/pallas_call | solution.py:424
  26.4 6.6 %x_solve.1 = (f32[3,3,16,192,128]{4,3,2,1,0:T(8,128)}, f32[3,16,192,128]{3,2,1,0:T(8,128)}) custom-call(f32[3,16,192,128]{3,2,1,0:T(8,128)S(1)} %get-tuple-element.9.v, f32[2,3,2,192,128]{4,3,2,1,0:T(8,128)S(1)} %get-tuple-element.10.xh, f32[2,6,192,128]{3,2,1,0:T(8,128)S(1)} %get-tuple-element.11.xp, f32[2,6,192,128]{3,2,1,0:T(8,128)S(1)} %get-tuple-element.12.xe, ...), custom_call_target="tpu_custom_call" | custom-call | tf_op jit(solution)/shard_map/x_solve/pallas_call | solution.py:518

commit v4 on v3

--- a/solution.py
+++ b/solution.py
@@ -14,6 +14,8 @@
 HIGH = lax.Precision.HIGHEST
 CHUNKS = 2
 OUT_CHUNKS = 6
+PLANES = 8
+EARLY = True
 MIB = 1 << 20
 
 
@@ -147,27 +149,30 @@
                     lines + [jnp.zeros((2, 128), F32)], axis=0)
 
 
-def z_local(p, v, parts, ztab, gyz, cyz, gather):
+def z_local(q, v, parts, ztab, gyz, cyz, gather):
     rows, cz = v.shape[2:]
     lane = iota((1, cz), 1)
-    for k in range(2):
-        x = 2 * p + k
+    planes = [PLANES * q + k for k in range(PLANES)]
+    for x in planes:
         velocity = [v[i, x] for i in range(3)]
         for field in range(6):
             value = velocity[field] if field < 3 else velocity[field - 3] * velocity[2]
             parts[field, x] = jnp.concatenate(split(value), axis=1)
+    ends = [gather[k * rows : (k + 1) * rows] for k in range(2)]
+    for k, x in enumerate(planes):
         got = dot(parts[:, x].reshape(6 * rows, 2 * cz), ztab[...])
         got = got[:, :cz] + got[:, cz:]
-        ends = gather[k * rows : (k + 1) * rows]
         for f in range(6):
             values = got[f * rows : (f + 1) * rows]
             if f < 3:
                 gyz[1, f, x] = values
             else:
                 cyz[f - 3, x] = values
-            first = 16 * p + 2 * f
-            ends = jnp.where((lane >= first) & (lane < first + 2), pltpu.roll(values, first + 1, 1), ends)
-        gather[k * rows : (k + 1) * rows] = ends
+            first = 8 * PLANES * q + 16 * (k // 2) + 2 * f
+            kept = (lane >= first) & (lane < first + 2)
+            ends[k % 2] = jnp.where(kept, pltpu.roll(values, first + 1, 1), ends[k % 2])
+    for k in range(2):
+        gather[k * rows : (k + 1) * rows] = ends[k]
 
 
 def beside(halo, near, far):
@@ -256,9 +261,9 @@
             xe[end, f, part] = ends[end][f]
 
 
-def along_y(p, v, parts, ytab, gyz, cyz):
+def along_y(q, v, parts, ytab, gyz, cyz):
     cz = v.shape[3]
-    planes = (2 * p, 2 * p + 1)
+    planes = [PLANES * q + k for k in range(PLANES)]
 
     def apply(pieces):
         high = jnp.concatenate([a[0] for a in pieces], axis=1)
@@ -276,6 +281,13 @@
         got = apply(held(4) if i == 2 else [split(v[i, x] * v[1, x]) for x in planes])
         for k, x in enumerate(planes):
             cyz[i, x] = cyz[i, x] + got[:, k * cz : (k + 1) * cz]
+
+
+def times(body, start, stop, unit):
+    @pl.loop(start // unit, stop // unit)
+    def _(t):
+        for k in range(unit):
+            body(unit * t + k)
 
 
 def exchange_kernel(
@@ -311,44 +323,47 @@
             src_ref=src, dst_ref=dst, send_sem=s, recv_sem=r, device_id=device, device_id_type=MESH)
 
     step = rows // CHUNKS
+    loads[0].wait()
+    loads[1].wait()
+    loads[6].wait()
+    z_inverse = zi[...]
+    corner = (z_inverse[0:1, 0:1], z_inverse[cz - 1 : cz, cz - 1 : cz])
+    z_weights(z_inverse, mz[...], ztab)
+    x_inverse = xi[...]
+    xcs[0] = jnp.broadcast_to(x_inverse[0:1, 0:1], (8, 128))
+    xcs[1] = jnp.broadcast_to(x_inverse[cx - 1 : cx, cx - 1 : cx], (8, 128))
+    x_end_weights(x_inverse, wtab)
+    loads[2].wait()
+    z_faces_of(v, corner, zs1)
+    if EARLY:
+        times(lambda t: x_local(t, v, wtab, xe), 0, rows // 8, 2)
+
     pl.semaphore_wait(barrier, 4)
     faces = []
     for c in range(CHUNKS):
         part = pl.ds(c * step, step)
         pair = (
-            send(v_hbm.at[:, pl.ds(cx - 2, 2), part], xh.at[0, :, :, part], x1s.at[0, c], x1r.at[0, c], right),
-            send(v_hbm.at[:, pl.ds(0, 2), part], xh.at[1, :, :, part], x1s.at[1, c], x1r.at[1, c], left),
+            send(v.at[:, pl.ds(cx - 2, 2), part], xh.at[0, :, :, part], x1s.at[0, c], x1r.at[0, c], right),
+            send(v.at[:, pl.ds(0, 2), part], xh.at[1, :, :, part], x1s.at[1, c], x1r.at[1, c], left),
         )
         for copy in pair:
             copy.start()
         faces.append(pair)
-
-    loads[0].wait()
-    loads[6].wait()
-    z_inverse = zi[...]
-    corner = (z_inverse[0:1, 0:1], z_inverse[cz - 1 : cz, cz - 1 : cz])
-    z_weights(z_inverse, mz[...], ztab)
-    loads[1].wait()
-    x_inverse = xi[...]
-    xcs[0] = jnp.broadcast_to(x_inverse[0:1, 0:1], (8, 128))
-    xcs[1] = jnp.broadcast_to(x_inverse[cx - 1 : cx, cx - 1 : cx], (8, 128))
     corners = (
         send(xcs.at[1], xc.at[0], xcsem.at[0], xcrecv.at[0], right),
         send(xcs.at[0], xc.at[1], xcsem.at[1], xcrecv.at[1], left),
     )
     for copy in corners:
         copy.start()
-    loads[2].wait()
-    z_faces_of(v, corner, zs1)
     z_faces = (
         send(zs1.at[1], zh.at[0], z1s.at[0], z1r.at[0], above),
         send(zs1.at[0], zh.at[1], z1s.at[1], z1r.at[1], below),
     )
     for copy in z_faces:
         copy.start()
-
-    x_end_weights(x_inverse, wtab)
-    pl.loop(0, rows // 8)(lambda t: x_local(t, v, wtab, xe))
+    if not EARLY:
+        times(lambda t: x_local(t, v, wtab, xe), 0, rows // 8, 2)
+
     inverse_metric = (1.0 / mz[:, 0:1], 1.0 / mz[:, cz - 1 : cz])
 
     def z_pass(first, last):
@@ -359,7 +374,7 @@
     def x_pass(c):
         for copy in faces[c]:
             copy.wait()
-        pl.loop(c * (step // 8), (c + 1) * (step // 8))(lambda t: x_halo(t, cx, xh, wtab, xe))
+        times(lambda t: x_halo(t, cx, xh, wtab, xe), c * (step // 8), (c + 1) * (step // 8), 2)
         part = pl.ds(c * step, step)
         pair = (
             send(xe.at[1, :, part], xp.at[0, :, part], x2s.at[0, c], x2r.at[0, c], right),
@@ -371,9 +386,7 @@
 
     z_tables(z_inverse, mz[...], spread)
     gather[...] = jnp.zeros(gather.shape, F32)
-    z_pass(0, cx // 4)
-    x_pass(0)
-    z_pass(cx // 4, cx // 2)
+    z_pass(0, cx // PLANES)
     for copy in z_faces:
         copy.wait()
     z_ends_of(gather, inverse_metric, zs2)
@@ -384,16 +397,21 @@
     )
     for copy in z_ends:
         copy.start()
-    for c in range(1, CHUNKS):
-        x_pass(c)
-
+    x_pass(0)
     for load in loads[3:6]:
         load.wait()
     ytab[...] = y_table(yi[...], my[...])
-    pl.loop(0, cx // 2)(lambda p: along_y(p, v, parts, ytab, gyz, cyz))
+
+    def y_pass(first, last):
+        pl.loop(first, last)(lambda q: along_y(q, v, parts, ytab, gyz, cyz))
+
+    y_pass(0, cx // 2 // PLANES)
+    for c in range(1, CHUNKS):
+        x_pass(c)
+    y_pass(cx // 2 // PLANES, cx // PLANES)
     for copy in z_ends:
         copy.wait()
-    pl.loop(0, cx // 4)(lambda q: z_correct(q, spread, z_inverse, zh, zp, zs2, gyz, cyz))
+    times(lambda q: z_correct(q, spread, z_inverse, zh, zp, zs2, gyz, cyz), 0, cx // 4, 2)
     for copy in corners:
         copy.wait()
     x_tables(x_inverse, mx[...], xc, tab)
@@ -496,10 +514,10 @@
         copy.start()
     step = rows // OUT_CHUNKS
     for c in range(OUT_CHUNKS):
-        @pl.loop(c * (step // 8), (c + 1) * (step // 8))
-        def _(t):
-            x_sweep(pl.ds(pl.multiple_of(t * 8, 8), 8), v, xh, xp, xe, tab, gx_out, conv_out, cyz)
-
+        times(
+            lambda t: x_sweep(
+                pl.ds(pl.multiple_of(t * 8, 8), 8), v, xh, xp, xe, tab, gx_out, conv_out, cyz),
+            c * (step // 8), (c + 1) * (step // 8), 2)
         part = pl.ds(c * step, step)
         pair = (
             pltpu.make_async_copy(gx_out.at[:, :, part], grad.at[:, 0, :, part], x_sem.at[c]),

time: 33.1 us -> 33 us (level)
  Pallas kernels: 32.3 us -> 31.9 us
    pallas_call x1, Pallas kernels: 25.7 us -> 25.4 us  [exchange(): pl.pallas_call(exchange_kernel, out_shape=tuple((jax.ShapeDtypeStruct(sha...]
where the time goes in v4:
time: 33 us; the launch traced here: 32.6 us
  Pallas kernels  31.9 us (97%)
  between operations  0.64 us (2%)
    pallas_call x1, Pallas kernels, exchange(): pl.pallas_call(exchange_kernel, out_shape=tuple((jax.ShapeDtypeStruct(sha...  25.4 us
    pallas_call x1, Pallas kernels, x_solve(): pl.pallas_call(x_kernel, out_shape=(jax.ShapeDtypeStruct((3, 3, cx, rows,...  6.58 us

profile of v4, /device:TPU:0, one launch (start us, length us, event | category | flops | bytes accessed | tf_op | source)
XLA Modules:
  0.0 32.6 jit_solution(10583421655150033127)
XLA Ops:
  0.6 25.4 %exchange.1 = (f32[3,16,192,128]{3,2,1,0:T(8,128)S(1)}, f32[2,3,2,192,128]{4,3,2,1,0:T(8,128)S(1)}, f32[2,6,192,128]{3,2,1,0:T(8,128)S(1)}, f32[2,6,192,128]{3,2...) custom-call(f32[3,16,192,128]{3,2,1,0:T(8,128)} %v_hbm.1, ...), custom_call_target="tpu_custom_call" | custom-call | tf_op jit(solution)/shard_map/exchange/pallas_call | solution.py:442
  26.0 6.6 %x_solve.1 = (f32[3,3,16,192,128]{4,3,2,1,0:T(8,128)}, f32[3,16,192,128]{3,2,1,0:T(8,128)}) custom-call(f32[3,16,192,128]{3,2,1,0:T(8,128)S(1)} %get-tuple-element.9.v, f32[2,3,2,192,128]{4,3,2,1,0:T(8,128)S(1)} %get-tuple-element.10.xh, f32[2,6,192,128]{3,2,1,0:T(8,128)S(1)} %get-tuple-element.11.xp, f32[2,6,192,128]{3,2,1,0:T(8,128)S(1)} %get-tuple-element.12.xe, ...), custom_call_target="tpu_custom_call" | custom-call | tf_op jit(solution)/shard_map/x_solve/pallas_call | solution.py:536

commit v5 on v4

--- a/solution.py
+++ b/solution.py
@@ -15,7 +15,6 @@
 CHUNKS = 2
 OUT_CHUNKS = 6
 PLANES = 8
-EARLY = True
 MIB = 1 << 20
 
 
@@ -323,6 +322,17 @@
             src_ref=src, dst_ref=dst, send_sem=s, recv_sem=r, device_id=device, device_id_type=MESH)
 
     step = rows // CHUNKS
+    pl.semaphore_wait(barrier, 4)
+    faces = []
+    for c in range(CHUNKS):
+        part = pl.ds(c * step, step)
+        pair = (
+            send(v_hbm.at[:, pl.ds(cx - 2, 2), part], xh.at[0, :, :, part], x1s.at[0, c], x1r.at[0, c], right),
+            send(v_hbm.at[:, pl.ds(0, 2), part], xh.at[1, :, :, part], x1s.at[1, c], x1r.at[1, c], left),
+        )
+        for copy in pair:
+            copy.start()
+        faces.append(pair)
     loads[0].wait()
     loads[1].wait()
     loads[6].wait()
@@ -335,20 +345,6 @@
     x_end_weights(x_inverse, wtab)
     loads[2].wait()
     z_faces_of(v, corner, zs1)
-    if EARLY:
-        times(lambda t: x_local(t, v, wtab, xe), 0, rows // 8, 2)
-
-    pl.semaphore_wait(barrier, 4)
-    faces = []
-    for c in range(CHUNKS):
-        part = pl.ds(c * step, step)
-        pair = (
-            send(v.at[:, pl.ds(cx - 2, 2), part], xh.at[0, :, :, part], x1s.at[0, c], x1r.at[0, c], right),
-            send(v.at[:, pl.ds(0, 2), part], xh.at[1, :, :, part], x1s.at[1, c], x1r.at[1, c], left),
-        )
-        for copy in pair:
-            copy.start()
-        faces.append(pair)
     corners = (
         send(xcs.at[1], xc.at[0], xcsem.at[0], xcrecv.at[0], right),
         send(xcs.at[0], xc.at[1], xcsem.at[1], xcrecv.at[1], left),
@@ -361,8 +357,7 @@
     )
     for copy in z_faces:
         copy.start()
-    if not EARLY:
-        times(lambda t: x_local(t, v, wtab, xe), 0, rows // 8, 2)
+    times(lambda t: x_local(t, v, wtab, xe), 0, rows // 8, 2)
 
     inverse_metric = (1.0 / mz[:, 0:1], 1.0 / mz[:, cz - 1 : cz])
 
@@ -386,7 +381,9 @@
 
     z_tables(z_inverse, mz[...], spread)
     gather[...] = jnp.zeros(gather.shape, F32)
-    z_pass(0, cx // PLANES)
+    z_pass(0, cx // 2 // PLANES)
+    x_pass(0)
+    z_pass(cx // 2 // PLANES, cx // PLANES)
     for copy in z_faces:
         copy.wait()
     z_ends_of(gather, inverse_metric, zs2)
@@ -397,7 +394,8 @@
     )
     for copy in z_ends:
         copy.start()
-    x_pass(0)
+    for c in range(1, CHUNKS):
+        x_pass(c)
     for load in loads[3:6]:
         load.wait()
     ytab[...] = y_table(yi[...], my[...])
@@ -405,10 +403,7 @@
     def y_pass(first, last):
         pl.loop(first, last)(lambda q: along_y(q, v, parts, ytab, gyz, cyz))
 
-    y_pass(0, cx // 2 // PLANES)
-    for c in range(1, CHUNKS):
-        x_pass(c)
-    y_pass(cx // 2 // PLANES, cx // PLANES)
+    y_pass(0, cx // PLANES)
     for copy in z_ends:
         copy.wait()
     times(lambda q: z_correct(q, spread, z_inverse, zh, zp, zs2, gyz, cyz), 0, cx // 4, 2)

time: 33 us -> 31 us (0.939)
  Pallas kernels: 31.9 us -> 30.2 us
    pallas_call x1, Pallas kernels: 25.4 us -> 23.7 us  [exchange(): pl.pallas_call(exchange_kernel, out_shape=tuple((jax.ShapeDtypeStruct(sha...]
where the time goes in v5:
time: 31 us; the launch traced here: 30.9 us
  Pallas kernels  30.2 us (97%)
  between operations  0.64 us (2%)
    pallas_call x1, Pallas kernels, exchange(): pl.pallas_call(exchange_kernel, out_shape=tuple((jax.ShapeDtypeStruct(sha...  23.7 us
    pallas_call x1, Pallas kernels, x_solve(): pl.pallas_call(x_kernel, out_shape=(jax.ShapeDtypeStruct((3, 3, cx, rows,...  6.58 us

profile of v5, /device:TPU:0, one launch (start us, length us, event | category | flops | bytes accessed | tf_op | source)
XLA Modules:
  0.0 30.9 jit_solution(15739440852301733774)
XLA Ops:
  0.6 23.7 %exchange.1 = (f32[3,16,192,128]{3,2,1,0:T(8,128)S(1)}, f32[2,3,2,192,128]{4,3,2,1,0:T(8,128)S(1)}, f32[2,6,192,128]{3,2,1,0:T(8,128)S(1)}, f32[2,6,192,128]{3,2...) custom-call(f32[3,16,192,128]{3,2,1,0:T(8,128)} %v_hbm.1, ...), custom_call_target="tpu_custom_call" | custom-call | tf_op jit(solution)/shard_map/exchange/pallas_call | solution.py:437
  24.3 6.6 %x_solve.1 = (f32[3,3,16,192,128]{4,3,2,1,0:T(8,128)}, f32[3,16,192,128]{3,2,1,0:T(8,128)}) custom-call(f32[3,16,192,128]{3,2,1,0:T(8,128)S(1)} %get-tuple-element.9.v, f32[2,3,2,192,128]{4,3,2,1,0:T(8,128)S(1)} %get-tuple-element.10.xh, f32[2,6,192,128]{3,2,1,0:T(8,128)S(1)} %get-tuple-element.11.xp, f32[2,6,192,128]{3,2,1,0:T(8,128)S(1)} %get-tuple-element.12.xe, ...), custom_call_target="tpu_custom_call" | custom-call | tf_op jit(solution)/shard_map/x_solve/pallas_call | solution.py:531

commit v6 on v5

--- a/solution.py
+++ b/solution.py
@@ -198,7 +198,7 @@
             zs2[side, p] = total
 
 
-def z_correct(q, spread, z_inverse, zh, zp, zs2, gyz, cyz):
+def z_correct(q, spread, z_inverse, zh, zp, zs2, gyz, cyz, gz_out, cyz_out):
     rows, cz = gyz.shape[3:]
     square = COUPLING * COUPLING
     own = (z_inverse[0:1, 0:1], z_inverse[cz - 1 : cz, cz - 1 : cz])
@@ -222,8 +222,8 @@
     more = dot(jnp.concatenate([turned, turned], axis=1), spread[...])
     planes = pl.ds(4 * q, 4)
     for i in range(3):
-        gyz[1, i, planes] = gyz[1, i, planes] + more[:, i * cz : (i + 1) * cz].reshape(4, rows, cz)
-        cyz[i, planes] = cyz[i, planes] + more[:, (3 + i) * cz : (4 + i) * cz].reshape(4, rows, cz)
+        gz_out[i, planes] = gyz[1, i, planes] + more[:, i * cz : (i + 1) * cz].reshape(4, rows, cz)
+        cyz_out[i, planes] = cyz[i, planes] + more[:, (3 + i) * cz : (4 + i) * cz].reshape(4, rows, cz)
 
 
 def x_local(t, v, wtab, xe):
@@ -291,8 +291,8 @@
 
 def exchange_kernel(
     v_hbm, xi_hbm, yi_hbm, zi_hbm, mx_hbm, my_hbm, mz_hbm,
-    v, xh, xp, xe, tab, gyz, cyz,
-    xi, yi, zi, mx, my, mz, xcs, xc, wtab, parts, zs1, zs2, zh, zp, gather, ytab, ztab, spread,
+    v, xh, xp, xe, tab, gyz, cyz, zi, zh, zp, zs2, spread,
+    xi, yi, mx, my, mz, xcs, xc, wtab, parts, zs1, gather, ytab, ztab,
     load_sem, x1s, x1r, x2s, x2r, z1s, z1r, z2s, z2r, xcsem, xcrecv,
 ):
     gx, gy, gz = lax.axis_index("gx"), lax.axis_index("gy"), lax.axis_index("gz")
@@ -406,7 +406,6 @@
     y_pass(0, cx // PLANES)
     for copy in z_ends:
         copy.wait()
-    times(lambda q: z_correct(q, spread, z_inverse, zh, zp, zs2, gyz, cyz), 0, cx // 4, 2)
     for copy in corners:
         copy.wait()
     x_tables(x_inverse, mx[...], xc, tab)
@@ -433,18 +432,21 @@
         (3 * cx + 32, 128),
         (2, 3, cx, rows, cz),
         (3, cx, rows, cz),
+        (cz, cz),
+        *[(2, cx // 2, 8, 2 * rows)] * 3,
     )
     return pl.pallas_call(
         exchange_kernel,
-        out_shape=tuple(jax.ShapeDtypeStruct(shape, F32) for shape in outs),
+        out_shape=tuple(jax.ShapeDtypeStruct(shape, F32) for shape in outs)
+        + (jax.ShapeDtypeStruct((256, 6 * cz), BF16),),
         in_specs=[pl.BlockSpec(memory_space=pltpu.HBM)] * 7,
-        out_specs=(pl.BlockSpec(memory_space=pltpu.VMEM),) * len(outs),
+        out_specs=(pl.BlockSpec(memory_space=pltpu.VMEM),) * (len(outs) + 1),
         scratch_shapes=[
-            vmem(cx, cx), vmem(rows, rows), vmem(cz, cz), vmem(1, cx), vmem(1, rows), vmem(1, cz),
+            vmem(cx, cx), vmem(rows, rows), vmem(1, cx), vmem(1, rows), vmem(1, cz),
             vmem(2, 8, 128), vmem(2, 8, 128), vmem(2 * (cx + 8), 128),
             half(6, cx, rows, 2 * cz),
-            *[vmem(2, cx // 2, 8, 2 * rows)] * 4, vmem(2 * rows, cz),
-            half(rows, 3 * rows), half(2 * cz, 2 * cz), half(256, 6 * cz),
+            vmem(2, cx // 2, 8, 2 * rows), vmem(2 * rows, cz),
+            half(rows, 3 * rows), half(2 * cz, 2 * cz),
             dma((7,)),
             dma((2, CHUNKS)), dma((2, CHUNKS)), dma((2, CHUNKS)), dma((2, CHUNKS)),
             dma((2,)), dma((2,)), dma((2,)), dma((2,)), dma((2,)), dma((2,)),
@@ -502,16 +504,26 @@
             conv[i, j, part] = state[3 + i] + cyz[i, j, part]
 
 
-def x_kernel(v, xh, xp, xe, tab, gyz, cyz, grad, conv, gx_out, conv_out, yz_sem, x_sem, c_sem):
+def x_kernel(
+    v, xh, xp, xe, tab, gyz, cyz, zi, zh, zp, zs2, spread, grad, conv,
+    gx_out, conv_out, gz_out, cyz_out, yz_sem, x_sem, c_sem,
+):
     rows = v.shape[2]
-    copies = [pltpu.make_async_copy(gyz.at[k], grad.at[:, 1 + k], yz_sem.at[k]) for k in range(2)]
-    for copy in copies:
-        copy.start()
+    copies = [
+        pltpu.make_async_copy(gyz.at[0], grad.at[:, 1], yz_sem.at[0]),
+        pltpu.make_async_copy(gz_out, grad.at[:, 2], yz_sem.at[1]),
+    ]
+    copies[0].start()
+    z_inverse = zi[...]
+    times(
+        lambda q: z_correct(q, spread, z_inverse, zh, zp, zs2, gyz, cyz, gz_out, cyz_out),
+        0, v.shape[1] // 4, 2)
+    copies[1].start()
     step = rows // OUT_CHUNKS
     for c in range(OUT_CHUNKS):
         times(
             lambda t: x_sweep(
-                pl.ds(pl.multiple_of(t * 8, 8), 8), v, xh, xp, xe, tab, gx_out, conv_out, cyz),
+                pl.ds(pl.multiple_of(t * 8, 8), 8), v, xh, xp, xe, tab, gx_out, conv_out, cyz_out),
             c * (step // 8), (c + 1) * (step // 8), 2)
         part = pl.ds(c * step, step)
         pair = (
@@ -525,8 +537,8 @@
         copy.wait()
 
 
-def x_solve(v, xh, xp, xe, tab, gyz, cyz):
-    _, cx, rows, cz = v.shape
+def x_solve(*arrays):
+    _, cx, rows, cz = arrays[0].shape
     dma = pltpu.SemaphoreType.DMA
     return pl.pallas_call(
         x_kernel,
@@ -534,16 +546,15 @@
             jax.ShapeDtypeStruct((3, 3, cx, rows, cz), F32),
             jax.ShapeDtypeStruct((3, cx, rows, cz), F32),
         ),
-        in_specs=[pl.BlockSpec(memory_space=pltpu.VMEM)] * 7,
+        in_specs=[pl.BlockSpec(memory_space=pltpu.VMEM)] * len(arrays),
         out_specs=(pl.BlockSpec(memory_space=pltpu.HBM),) * 2,
         scratch_shapes=[
-            pltpu.VMEM((3, cx, rows, cz), F32),
-            pltpu.VMEM((3, cx, rows, cz), F32),
+            *[pltpu.VMEM((3, cx, rows, cz), F32)] * 4,
             dma((2,)), dma((OUT_CHUNKS,)), dma((OUT_CHUNKS,)),
         ],
-        compiler_params=pltpu.CompilerParams(vmem_limit_bytes=14 * MIB),
+        compiler_params=pltpu.CompilerParams(vmem_limit_bytes=24 * MIB),
         name="x_solve",
-    )(v, xh, xp, xe, tab, gyz, cyz)
+    )(*arrays)
 
 
 def on_device(velocity, metric_x, metric_y, metric_z, x_inverse, y_inverse, z_inverse):

time: 31 us -> 32 us (1.032)
  Pallas kernels: 30.2 us -> 31.2 us
    pallas_call x1, Pallas kernels: 6.58 us -> 8.1 us  [x_solve(): pl.pallas_call(x_kernel, out_shape=(jax.ShapeDtypeStruct((3, 3, cx, rows,...]
    pallas_call x1, Pallas kernels: 23.7 us -> 23.1 us  [exchange(): pl.pallas_call(exchange_kernel, out_shape=tuple((jax.ShapeDtypeStruct(sha...]
where the time goes in v6:
time: 32 us; the launch traced here: 31.8 us
  Pallas kernels  31.2 us (98%)
  between operations  0.64 us (2%)
    pallas_call x1, Pallas kernels, exchange(): pl.pallas_call(exchange_kernel, out_shape=tuple((jax.ShapeDtypeStruct(sha...  23.1 us
    pallas_call x1, Pallas kernels, x_solve(): pl.pallas_call(x_kernel, out_shape=(jax.ShapeDtypeStruct((3, 3, cx, rows,...  8.1 us

profile of v6, /device:TPU:0, one launch (start us, length us, event | category | flops | bytes accessed | tf_op | source)
XLA Modules:
  0.0 31.8 jit_solution(16911961008915686498)
XLA Ops:
  0.6 23.1 %exchange.1 = (f32[3,16,192,128]{3,2,1,0:T(8,128)S(1)}, f32[2,3,2,192,128]{4,3,2,1,0:T(8,128)S(1)}, f32[2,6,192,128]{3,2,1,0:T(8,128)S(1)}, f32[2,6,192,128]{3,2...) custom-call(f32[3,16,192,128]{3,2,1,0:T(8,128)} %v_hbm.1, ...), custom_call_target="tpu_custom_call" | custom-call | tf_op jit(solution)/shard_map/exchange/pallas_call | solution.py:438
  23.7 8.1 %x_solve.1 = (f32[3,3,16,192,128]{4,3,2,1,0:T(8,128)}, f32[3,16,192,128]{3,2,1,0:T(8,128)}) custom-call(f32[3,16,192,128]{3,2,1,0:T(8,128)S(1)} %get-tuple-element.14.v, f32[2,3,2,192,128]{4,3,2,1,0:T(8,128)S(1)} %get-tuple-element.15.xh, f32[2,6,192,128]{3,2,1,0:T(8,128)S(1)} %get-tuple-element.16.xp, f32[2,6,192,128]{3,2,1,0:T(8,128)S(1)} %get-tuple-element.17.xe, ...), custom_call_target="tpu_custom_call" | custom-call | tf_op jit(solution)/shard_map/x_solve/pallas_call | solution.py:543

commit v7 on v5

--- a/solution.py
+++ b/solution.py
@@ -12,7 +12,7 @@
 BF16 = jnp.bfloat16
 MESH = pl.DeviceIdType.MESH
 HIGH = lax.Precision.HIGHEST
-CHUNKS = 2
+CHUNKS = 4
 OUT_CHUNKS = 6
 PLANES = 8
 MIB = 1 << 20
@@ -383,7 +383,9 @@
     gather[...] = jnp.zeros(gather.shape, F32)
     z_pass(0, cx // 2 // PLANES)
     x_pass(0)
+    x_pass(1)
     z_pass(cx // 2 // PLANES, cx // PLANES)
+    x_pass(2)
     for copy in z_faces:
         copy.wait()
     z_ends_of(gather, inverse_metric, zs2)
@@ -394,7 +396,7 @@
     )
     for copy in z_ends:
         copy.start()
-    for c in range(1, CHUNKS):
+    for c in range(3, CHUNKS):
         x_pass(c)
     for load in loads[3:6]:
         load.wait()

time: 31 us -> 31.1 us (level)
  no operation moved by 1% of the time
where the time goes in v7:
time: 31.1 us; the launch traced here: 30.9 us
  Pallas kernels  30.3 us (97%)
  between operations  0.64 us (2%)
    pallas_call x1, Pallas kernels, exchange(): pl.pallas_call(exchange_kernel, out_shape=tuple((jax.ShapeDtypeStruct(sha...  23.7 us
    pallas_call x1, Pallas kernels, x_solve(): pl.pallas_call(x_kernel, out_shape=(jax.ShapeDtypeStruct((3, 3, cx, rows,...  6.58 us

profile of v7, /device:TPU:0, one launch (start us, length us, event | category | flops | bytes accessed | tf_op | source)
XLA Modules:
  0.0 30.9 jit_solution(15465487752029107607)
XLA Ops:
  0.6 23.7 %exchange.1 = (f32[3,16,192,128]{3,2,1,0:T(8,128)S(1)}, f32[2,3,2,192,128]{4,3,2,1,0:T(8,128)S(1)}, f32[2,6,192,128]{3,2,1,0:T(8,128)S(1)}, f32[2,6,192,128]{3,2...) custom-call(f32[3,16,192,128]{3,2,1,0:T(8,128)} %v_hbm.1, ...), custom_call_target="tpu_custom_call" | custom-call | tf_op jit(solution)/shard_map/exchange/pallas_call | solution.py:439
  24.4 6.6 %x_solve.1 = (f32[3,3,16,192,128]{4,3,2,1,0:T(8,128)}, f32[3,16,192,128]{3,2,1,0:T(8,128)}) custom-call(f32[3,16,192,128]{3,2,1,0:T(8,128)S(1)} %get-tuple-element.9.v, f32[2,3,2,192,128]{4,3,2,1,0:T(8,128)S(1)} %get-tuple-element.10.xh, f32[2,6,192,128]{3,2,1,0:T(8,128)S(1)} %get-tuple-element.11.xp, f32[2,6,192,128]{3,2,1,0:T(8,128)S(1)} %get-tuple-element.12.xe, ...), custom_call_target="tpu_custom_call" | custom-call | tf_op jit(solution)/shard_map/x_solve/pallas_call | solution.py:533
